TPU v7x, 128 devices: a whole 4x4x4 slice. The times are simulated.
128 devices in a mesh: ctx: 8 (over x_lo, z), fsdp: 16 (over y, x_hi, core).
Axes of the slice: x: 4 (x_hi: 2, x_lo: 2; x = x_hi * 2 + x_lo), y: 4, z: 4, core: 2. Of those that a mesh axis runs over, the one named last changes fastest.
Arguments:
- queries: bfloat16 [16, 1536, 2048], P('fsdp', 'ctx'), may hold values from -5 to 5
- keys: bfloat16 [16, 1536, 2048], P('fsdp', 'ctx'), may hold values from -5 to 5
- values: bfloat16 [16, 1536, 2048], P('fsdp', 'ctx'), may hold values from -6 to 6
- resid: float32 [16, 1536, 4096], P('fsdp', 'ctx'), may hold values from -6 to 6
- gate: float32 [16, 4096], P('fsdp'), may hold values from 0.5 to 1.5
- out_weight: bfloat16 [2048, 4096], P(('ctx', 'fsdp')), may hold values from -2 to 2
- conv_weight: float32 [3, 4096], replicated, may hold values from -2.5 to 2.5
- cotangent: float32 [16, 1536, 4096], P('fsdp', 'ctx'), may hold values from -6 to 6
Outputs:
- encoded: float32 [16, 1536, 4096], P('fsdp', 'ctx')
- grad_queries: bfloat16 [16, 1536, 2048], P('fsdp', 'ctx')
- grad_keys: bfloat16 [16, 1536, 2048], P('fsdp', 'ctx')
- grad_values: bfloat16 [16, 1536, 2048], P('fsdp', 'ctx')
- grad_conv: float32 [3, 4096], replicated
All inputs are finite; a program needn't handle non-finite values.
Results may differ from a plain program's by a relative error of at most 0.019.
Values may be sent and summed in bfloat16 or wider, within the bound.
No kernel may reach another device: no remote copies, remote signals or barrier semaphores. Data moves between devices by JAX's collectives and lax.ppermute only.
A program may use at most 192 MiB of HBM per device.

v0:
```python
import math

import jax
import jax.numpy as jnp
import numpy as np
from jax import lax
from jax.experimental import pallas as pl
from jax.experimental.pallas import tpu as pltpu
from jax.sharding import PartitionSpec as P


HDIM = 128
KSIZE = 3
TOKF = 48
CTX = 8
PARTS = 12
ROWS = 192
SEQ = CTX * ROWS
HW = 2048
D = 4096
HALF = D // 2
SPAN = (KSIZE - 1) * TOKF
PIECE = HW // CTX
BLOCK = 256
FACTOR = 1.0 / math.sqrt(HDIM)
LOG2E = math.log2(math.e)
AXES = ("ctx", "fsdp")
bf16 = jnp.bfloat16
f32 = jnp.float32


def coords(flat):
    ctx, fsdp = divmod(flat, 16)
    x_lo, z = divmod(ctx, 4)
    y, rest = divmod(fsdp, 4)
    x_hi, core = divmod(rest, 2)
    return dict(x=x_hi * 2 + x_lo, y=y, z=z, core=core)


def flat_of(place):
    x_hi, x_lo = divmod(place["x"], 2)
    return (x_lo * 4 + place["z"]) * 16 + place["y"] * 4 + x_hi * 2 + place["core"]


def shift(array, dim, by):
    size = 2 if dim == "core" else 4
    pairs = []
    for source in range(128):
        place = coords(source)
        place[dim] = (place[dim] + by) % size
        pairs.append((source, flat_of(place)))
    return lax.ppermute(array, AXES, pairs)


def swap(array, axis, key):
    count = lax.axis_size(axis)
    return lax.ppermute(array, axis, [(i, i ^ key) for i in range(count)])


def along(array, by):
    pairs = [(i, i + by) for i in range(CTX) if 0 <= i + by < CTX]
    return lax.ppermute(array, "ctx", pairs)


def moved(offsets, dim, by):
    return [dict(o, **{dim: o[dim] - by}) for o in offsets]


def gather_rows(rows):
    got = [(rows, [dict(x=0, y=0, z=0)])]
    for by in (1, -1, 2):
        got.append((shift(rows, "z", by), moved(got[0][1], "z", by)))
    plane = jnp.concatenate([g[0] for g in got], axis=0)
    offs = [o for g in got for o in g[1]]
    got = [(plane, offs)]
    for by in (1, -1, 2):
        got.append((shift(plane, "x", by), moved(offs, "x", by)))
    far = jnp.concatenate([got[2][0], got[3][0]], axis=0)
    got = got[:2] + [(far, got[2][1] + got[3][1])]
    ups, downs, out = {}, {}, list(got)
    ups[0] = shift(plane, "y", 1)
    downs[0] = shift(plane, "y", -1)
    for up, down in ((1, 2), (2, 1)):
        ups[up] = shift(got[up][0], "y", 1)
        downs[down] = shift(got[down][0], "y", -1)
    twice = [shift(ups[0], "y", 1), shift(ups[1], "y", 1), shift(downs[2], "y", -1)]
    for place in range(3):
        out.append((ups[place], moved(got[place][1], "y", 1)))
        out.append((downs[place], moved(got[place][1], "y", -1)))
        out.append((twice[place], moved(got[place][1], "y", 2)))
    return out


def params(mib=56):
    return pltpu.CompilerParams(vmem_limit_bytes=mib * 2**20)


SMEM = pl.BlockSpec(memory_space=pltpu.SMEM)
VMEM = pl.BlockSpec(memory_space=pltpu.VMEM)
ANY = pl.BlockSpec(memory_space=pl.ANY)


def shape(dims, dtype):
    return jax.ShapeDtypeStruct(dims, dtype)


def pack_body(ids, q_ref, k_ref, v_ref, *outs):
    for key in range(CTX):
        start = pl.multiple_of((ids[0] ^ key) * PIECE, PIECE)
        for place, ref in enumerate((q_ref, k_ref, v_ref)):
            outs[key][:, place * PIECE : (place + 1) * PIECE] = ref[:, pl.ds(start, PIECE)]


def pack(ids, queries, keys, values):
    return pl.pallas_call(
        pack_body,
        in_specs=[SMEM, VMEM, VMEM, VMEM],
        out_specs=[VMEM] * CTX,
        out_shape=[shape((ROWS, 3 * PIECE), bf16)] * CTX,
        compiler_params=params(10),
        name="pack",
    )(ids, queries, keys, values)


def forward_body(*refs):
    pieces, refs = refs[:CTX], refs[CTX:]
    outs, refs = refs[:CTX], refs[CTX:]
    log_ref, q_s, k_s, v_s, o_s = refs
    for head in range(2):
        for key in range(CTX):
            rows = slice(key * ROWS, (key + 1) * ROWS)
            for place, ref in enumerate((q_s, k_s, v_s)):
                start = place * PIECE + head * HDIM
                ref[head, rows, :] = pieces[key][:, start : start + HDIM]

    def step(index, carry):
        head = index // (SEQ // BLOCK)
        start = pl.multiple_of((index % (SEQ // BLOCK)) * BLOCK, BLOCK)
        query = q_s[head, pl.ds(start, BLOCK), :]
        scores = lax.dot_general(
            query, k_s[head], (((1,), (1,)), ((), ())), preferred_element_type=f32
        )
        peak = jnp.max(scores, axis=1, keepdims=True)
        raised = jnp.exp2((scores - peak) * (FACTOR * LOG2E))
        totals = jnp.sum(raised, axis=1, keepdims=True)
        summed = jnp.dot(raised.astype(bf16), v_s[head], preferred_element_type=f32)
        o_s[head, pl.ds(start, BLOCK), :] = (summed / totals).astype(bf16)
        logs = peak * (FACTOR * LOG2E) + jnp.log2(totals)
        log_ref[head, :, pl.ds(start, BLOCK)] = jnp.broadcast_to(logs, (BLOCK, HDIM)).T[:8]
        return carry

    lax.fori_loop(0, 2 * SEQ // BLOCK, step, 0)
    for key in range(CTX):
        rows = slice(key * ROWS, (key + 1) * ROWS)
        outs[key][:, :HDIM] = o_s[0, rows, :]
        outs[key][:, HDIM:] = o_s[1, rows, :]


def forward(pieces):
    return pl.pallas_call(
        forward_body,
        in_specs=[VMEM] * CTX,
        out_specs=[VMEM] * (CTX + 1),
        out_shape=[shape((ROWS, PIECE), bf16)] * CTX + [shape((2, 8, SEQ), f32)],
        scratch_shapes=[pltpu.VMEM((2, SEQ, HDIM), bf16)] * 4,
        compiler_params=params(24),
        name="attend",
    )(*pieces)


def backward_body(head, *refs):
    pieces, refs = refs[:CTX], refs[CTX:]
    att, refs = refs[:CTX], refs[CTX:]
    grads, refs = refs[:CTX], refs[CTX:]
    log_ref, refs = refs[0], refs[1:]
    outs, refs = refs[:CTX], refs[CTX:]
    q_s, k_s, v_s, g_s, d_s, kt_s, dq_s, dk_s, dv_s = refs
    cols = slice(head * HDIM, (head + 1) * HDIM)
    for key in range(CTX):
        rows = slice(key * ROWS, (key + 1) * ROWS)
        for place, ref in enumerate((q_s, k_s, v_s)):
            start = place * PIECE + head * HDIM
            ref[rows, :] = pieces[key][:, start : start + HDIM]
        grad = grads[key][:, cols]
        g_s[rows, :] = grad
        d_s[rows, :] = grad.astype(f32) * att[key][:, cols].astype(f32)
    kt_s[...] = k_s[...].astype(f32).T.astype(bf16)
    dk_s[...] = jnp.zeros_like(dk_s)
    dv_s[...] = jnp.zeros_like(dv_s)
    wide = 512

    def step(index, carry):
        start = pl.multiple_of(index * BLOCK, BLOCK)
        query = q_s[pl.ds(start, BLOCK), :]
        grad = g_s[pl.ds(start, BLOCK), :]
        delta = jnp.sum(d_s[pl.ds(start, BLOCK), :].T, axis=0, keepdims=True)
        logs = log_ref[head, 0:1, pl.ds(start, BLOCK)]
        dq = jnp.zeros((HDIM, BLOCK), f32)
        for chunk in range(SEQ // wide):
            part = slice(chunk * wide, (chunk + 1) * wide)
            scores = lax.dot_general(
                k_s[part, :], query, (((1,), (1,)), ((), ())), preferred_element_type=f32
            )
            dprob = lax.dot_general(
                v_s[part, :], grad, (((1,), (1,)), ((), ())), preferred_element_type=f32
            )
            probs = jnp.exp2(scores * (FACTOR * LOG2E) - logs)
            dscore = (probs * (dprob - delta)).astype(bf16)
            dv_s[part, :] += jnp.dot(probs.astype(bf16), grad, preferred_element_type=f32)
            dk_s[part, :] += jnp.dot(dscore, query, preferred_element_type=f32)
            dq = dq + jnp.dot(kt_s[:, part], dscore, preferred_element_type=f32)
        dq_s[pl.ds(start, BLOCK), :] = (dq.T * FACTOR).astype(bf16)
        return carry

    lax.fori_loop(0, SEQ // BLOCK, step, 0)
    for key in range(CTX):
        rows = slice(key * ROWS, (key + 1) * ROWS)
        outs[key][:, :HDIM] = dq_s[rows, :]
        outs[key][:, HDIM : 2 * HDIM] = (dk_s[rows, :] * FACTOR).astype(bf16)
        outs[key][:, 2 * HDIM :] = dv_s[rows, :].astype(bf16)


def backward(head, pieces, att, grads, logs):
    return pl.pallas_call(
        lambda *refs: backward_body(head, *refs),
        in_specs=[VMEM] * (3 * CTX + 1),
        out_specs=[VMEM] * CTX,
        out_shape=[shape((ROWS, 3 * HDIM), bf16)] * CTX,
        scratch_shapes=[pltpu.VMEM((SEQ, HDIM), bf16)] * 4
        + [
            pltpu.VMEM((SEQ, HDIM), f32),
            pltpu.VMEM((HDIM, SEQ), bf16),
            pltpu.VMEM((SEQ, HDIM), bf16),
            pltpu.VMEM((SEQ, HDIM), f32),
            pltpu.VMEM((SEQ, HDIM), f32),
        ],
        compiler_params=params(24),
    )(*pieces, *att, *grads, logs)


def load_rows(table, arrays, runs, rows_s, sems):
    for place, (which, row) in enumerate(runs):
        target = pl.multiple_of(table[place], 32)
        block = lax.shift_right_logical(table[place], 8)
        pltpu.make_async_copy(
            arrays[which].at[pl.ds(row, 32), :], rows_s.at[pl.ds(target, 32), :], sems.at[block]
        ).start()


def wait_rows(key, rows_s, sems):
    rows = rows_s.at[pl.ds(pl.multiple_of(key * PIECE, PIECE), PIECE), :]
    pltpu.make_async_copy(rows, rows, sems.at[key]).wait()


def project_back_body(runs, table, own_ref, other_ref, *refs):
    arrays, refs = refs[:PARTS], refs[PARTS:]
    keep_ref, send_ref, rows_s, sems, grad_s = refs
    load_rows(table, arrays, runs, rows_s, sems)
    grad_s[0:ROWS, :] = own_ref[...]
    grad_s[ROWS:, :] = other_ref[...]

    def step(key, carry):
        wait_rows(key, rows_s, sems)
        out = lax.dot_general(
            grad_s[...],
            rows_s[pl.ds(pl.multiple_of(key * PIECE, PIECE), PIECE), :],
            (((1,), (1,)), ((), ())),
            preferred_element_type=f32,
        )
        keep_ref[key] = out[:ROWS]
        send_ref[key] = out[ROWS:].astype(bf16)
        return carry

    lax.fori_loop(0, CTX, step, 0)


def project_back(runs, table, own, other, arrays):
    return pl.pallas_call(
        lambda *refs: project_back_body(runs, *refs),
        in_specs=[SMEM, VMEM, VMEM] + [ANY] * PARTS,
        out_specs=[VMEM, VMEM],
        out_shape=[shape((CTX, ROWS, PIECE), f32), shape((CTX, ROWS, PIECE), bf16)],
        scratch_shapes=[
            pltpu.VMEM((HW, HALF), bf16),
            pltpu.SemaphoreType.DMA((CTX,)),
            pltpu.VMEM((2 * ROWS, HALF), bf16),
        ],
        compiler_params=params(32),
        name="project_back",
    )(table, own, other, *arrays)


def project_body(runs, table, *refs):
    own, other, refs = refs[0], refs[1], refs[2:]
    arrays, refs = refs[:PARTS], refs[PARTS:]
    keep_ref, send_ref, rows_s, sems, att_s, sum_s = refs
    load_rows(table, arrays, runs, rows_s, sems)
    for key in range(CTX):
        att_s[key, 0:ROWS, :] = own[key]
        att_s[key, ROWS:, :] = other[key]
    sum_s[...] = jnp.zeros_like(sum_s)

    def step(key, carry):
        wait_rows(key, rows_s, sems)
        sum_s[...] += jnp.dot(
            att_s[key],
            rows_s[pl.ds(pl.multiple_of(key * PIECE, PIECE), PIECE), :],
            preferred_element_type=f32,
        )
        return carry

    lax.fori_loop(0, CTX, step, 0)
    keep_ref[...] = sum_s[0:ROWS, :]
    send_ref[...] = sum_s[ROWS:, :].astype(bf16)


def project(runs, table, own, other, arrays):
    return pl.pallas_call(
        lambda *refs: project_body(runs, *refs),
        in_specs=[SMEM] + [VMEM] * 2 + [ANY] * PARTS,
        out_specs=[VMEM, VMEM],
        out_shape=[shape((ROWS, HALF), f32), shape((ROWS, HALF), bf16)],
        scratch_shapes=[
            pltpu.VMEM((HW, HALF), bf16),
            pltpu.SemaphoreType.DMA((CTX,)),
            pltpu.VMEM((CTX, 2 * ROWS, PIECE), bf16),
            pltpu.VMEM((2 * ROWS, HALF), f32),
        ],
        compiler_params=params(32),
        name="project",
    )(table, own, other, *arrays)


def stack_body(*refs):
    for key in range(CTX):
        refs[CTX][key] = refs[key][...]


def stack(pieces):
    return pl.pallas_call(
        stack_body,
        in_specs=[VMEM] * CTX,
        out_specs=VMEM,
        out_shape=shape((CTX, ROWS, PIECE), bf16),
        compiler_params=params(10),
        name="stack",
    )(*pieces)


def join_body(keep_ref, got_ref, *outs):
    for key in range(CTX):
        outs[key][...] = (keep_ref[key] + got_ref[key].astype(f32)).astype(bf16)


def join(keep, got):
    return pl.pallas_call(
        join_body,
        in_specs=[VMEM, VMEM],
        out_specs=[VMEM] * CTX,
        out_shape=[shape((ROWS, PIECE), bf16)] * CTX,
        compiler_params=params(10),
        name="join",
    )(keep, got)


COLS = 512
STEPS = HALF // COLS


def grad_proj_body(ids, *refs):
    ins, outs = refs[:8], refs[8:]
    for side in range(2):
        cot_ref, later_ref, gate_ref, conv_ref = ins[4 * side : 4 * side + 4]
        cot = cot_ref[...]
        ext = jnp.concatenate([cot, later_ref[...].astype(f32)], axis=0)
        grad = cot
        for offset in range(KSIZE):
            grad = grad + conv_ref[offset : offset + 1, :] * ext[offset * TOKF : offset * TOKF + ROWS]
        outs[side][...] = (gate_ref[...] * grad).astype(bf16)


def grad_proj(ids, cot, later, gate, conv):
    def spec(rows, side):
        return pl.BlockSpec((rows, COLS), lambda i, ids: (0, (ids[1] ^ side) * STEPS + i))

    ins = []
    for side in range(2):
        ins += [spec(ROWS, side), spec(SPAN, side), spec(1, side), spec(KSIZE, side)]
    return pl.pallas_call(
        grad_proj_body,
        grid_spec=pltpu.PrefetchScalarGridSpec(
            num_scalar_prefetch=1,
            grid=(STEPS,),
            in_specs=ins,
            out_specs=[pl.BlockSpec((ROWS, COLS), lambda i, ids: (0, i))] * 2,
        ),
        out_shape=[shape((ROWS, HALF), bf16)] * 2,
        compiler_params=params(16),
        name="grad_proj",
    )(ids, *([cot, later, gate, conv] * 2))


def mix_body(ids, resid_ref, gate_ref, keep_ref, got_ref, mixed_ref, tail_ref):
    near = pl.program_id(0) < STEPS
    projected = jnp.where(near, keep_ref[...], got_ref[...].astype(f32))
    mixed = (resid_ref[...] + gate_ref[...] * projected).astype(bf16)
    mixed_ref[...] = mixed
    tail_ref[...] = mixed[ROWS - SPAN :]


def mix(ids, resid, gate, keep, got):
    def full(i, ids):
        return (0, (ids[1] ^ (i // STEPS)) * STEPS + i % STEPS)

    return pl.pallas_call(
        mix_body,
        grid_spec=pltpu.PrefetchScalarGridSpec(
            num_scalar_prefetch=1,
            grid=(2 * STEPS,),
            in_specs=[
                pl.BlockSpec((ROWS, COLS), full),
                pl.BlockSpec((1, COLS), full),
                pl.BlockSpec((ROWS, COLS), lambda i, ids: (0, jnp.minimum(i, STEPS - 1))),
                pl.BlockSpec((ROWS, COLS), lambda i, ids: (0, jnp.maximum(i, STEPS) - STEPS)),
            ],
            out_specs=[pl.BlockSpec((ROWS, COLS), full), pl.BlockSpec((SPAN, COLS), full)],
        ),
        out_shape=[shape((ROWS, D), bf16), shape((SPAN, D), bf16)],
        compiler_params=params(16),
        name="mix",
    )(ids, resid, gate, keep, got)


def encode_body(mixed_ref, prior_ref, conv_ref, cot_ref, out_ref, sum_ref):
    mixed = mixed_ref[...].astype(f32)
    ext = jnp.concatenate([prior_ref[...].astype(f32), mixed], axis=0)
    cot = cot_ref[...]
    encoded = mixed
    for offset in range(KSIZE):
        begin = SPAN - offset * TOKF
        earlier = ext[begin : begin + ROWS]
        encoded = encoded + conv_ref[offset : offset + 1, :] * earlier
        row = offset * (D // COLS) + pl.program_id(0)
        sum_ref[pl.ds(row, 1), :] = jnp.sum(cot * earlier, axis=0, keepdims=True)
    out_ref[...] = encoded


def encode(mixed, prior, conv, cot):
    def spec(rows):
        return pl.BlockSpec((rows, COLS), lambda i: (0, i))

    return pl.pallas_call(
        encode_body,
        grid=(D // COLS,),
        in_specs=[spec(ROWS), spec(SPAN), spec(KSIZE), spec(ROWS)],
        out_specs=[spec(ROWS), pl.BlockSpec((KSIZE * D // COLS, COLS), lambda i: (0, 0))],
        out_shape=[shape((ROWS, D), f32), shape((KSIZE * D // COLS, COLS), f32)],
        compiler_params=params(16),
        name="encode",
    )(mixed, prior, conv, cot)


def unpack_body(ids, *refs):
    groups, outs = (refs[:CTX], refs[CTX : 2 * CTX]), refs[2 * CTX :]
    for key in range(CTX):
        for head, group in enumerate(groups):
            start = pl.multiple_of((ids[0] ^ key) * PIECE + head * HDIM, HDIM)
            for place in range(3):
                part = slice(place * HDIM, (place + 1) * HDIM)
                outs[place][:, pl.ds(start, HDIM)] = group[key][:, part]


def unpack(ids, firsts, seconds):
    return pl.pallas_call(
        unpack_body,
        in_specs=[SMEM] + [VMEM] * (2 * CTX),
        out_specs=[VMEM] * 3,
        out_shape=[shape((ROWS, HW), bf16)] * 3,
        compiler_params=params(12),
        name="unpack",
    )(ids, *firsts, *seconds)


def exchange(pieces, keys=range(1, CTX)):
    got = [swap(pieces[key], "ctx", key) for key in keys]
    return got if keys[0] > 1 else [pieces[0]] + got


def exchange_in(pieces, groups):
    got = []
    for keys in groups:
        got += exchange(pieces, range(*keys))
    return got


def after(values, *others):
    return lax.optimization_barrier((values, others))[0]


def add_swap(sums, axis, mask):
    return sums + swap(sums, axis, mask)


def block(queries, keys, values, resid, gate, out_weight, conv_weight, cotangent):
    ctx = lax.axis_index("ctx")
    fsdp = lax.axis_index("fsdp")
    core = fsdp % 2
    ids = jnp.stack([ctx, core]).astype(jnp.int32)

    other_rows = shift(out_weight, "core", 1)
    mine = lax.dynamic_slice(out_weight, (0, core * HALF), (16, HALF))
    theirs = lax.dynamic_slice(other_rows, (0, core * HALF), (16, HALF))
    rows = jnp.where(
        core == 0,
        jnp.concatenate([mine, theirs], axis=0),
        jnp.concatenate([theirs, mine], axis=0),
    )
    gathered = gather_rows(rows)
    arrays = [g[0] for g in gathered]
    runs = []
    for which, (_, offs) in enumerate(gathered):
        for place, off in enumerate(offs):
            runs.append((off["z"] % 4, off["x"] % 2, which, place * 32, off))
    runs.sort(key=lambda run: run[:4])
    dx, dy, dz = (np.array([run[4][d] for run in runs], np.int32) for d in "xyz")
    x_lo, z = ctx // 4, ctx % 4
    x = (fsdp // 2 % 2) * 2 + x_lo
    run_x = (x + dx) % 4
    run_y = (fsdp // 4 + dy) % 4
    run_z = (z + dz) % 4
    block = ((run_x % 2) ^ x_lo) * 4 + (run_z ^ z)
    table = (block * PIECE + run_y * 64 + (run_x // 2) * 32).astype(jnp.int32)
    runs = [run[2:4] for run in runs]

    packed = pack(ids, queries[0], keys[0], values[0])
    pieces = exchange(packed, range(1, 4))
    pieces += exchange(packed, range(4, CTX))
    later = along(cotangent[0, :SPAN].astype(bf16), -1)
    results = forward(after(pieces, arrays[0], arrays[1]))
    att, logs = results[:CTX], results[CTX]
    own_att = exchange(att)
    own_grad, send_grad = grad_proj(ids, cotangent[0], later, gate, conv_weight)
    other_grad = shift(send_grad, "core", 1)
    keep, send = project_back(runs, table, own_grad, other_grad, arrays)
    got = shift(send, "core", 1)
    own_att = stack(own_att)
    other_att = shift(own_att, "core", 1)
    joined = join(keep, got)
    grads = exchange(joined)

    keep, send = project(runs, table, after(own_att, joined[0]), other_att, arrays)
    mixed, tail = mix(ids, resid[0], gate, keep, shift(send, "core", 1))
    prior = along(tail, 1)

    firsts = backward(0, pieces, att, after(grads, tail), logs)
    encoded, sums = encode(mixed, prior, conv_weight, after(cotangent[0], firsts[0]))
    sums = add_swap(sums, "fsdp", 1)
    early = exchange_in(firsts, ((1, 4), (4, 8)))
    sums = add_swap(sums, "fsdp", 4)
    sums = add_swap(sums, "fsdp", 8)
    seconds = backward(1, pieces, att, grads, logs)
    sums = add_swap(after(sums, seconds[0]), "fsdp", 2)
    late = exchange_in(seconds, ((1, 3), (3, 6), (6, 8)))
    sums = add_swap(sums, "ctx", 4)
    sums = add_swap(sums, "ctx", 1)
    sums = add_swap(sums, "ctx", 2)
    grad_conv = sums.reshape(KSIZE, D)
    grad_q, grad_k, grad_v = unpack(ids, early, late)
    return (encoded[None], grad_q[None], grad_k[None], grad_v[None], grad_conv)


def solution(mesh):
    token = P("fsdp", "ctx", None)
    in_specs = (
        token,
        token,
        token,
        token,
        P("fsdp", None),
        P(("ctx", "fsdp"), None),
        P(),
        token,
    )
    return jax.shard_map(
        block,
        mesh=mesh,
        in_specs=in_specs,
        out_specs=(token, token, token, token, P()),
        check_vma=False,
    )
```

profile of v0, /device:TPU:0, one launch (start us, length us, event | category | flops | bytes accessed | tf_op | source)
XLA Modules:
  0.0 281.3 jit_solution(6759010114268598830)
XLA Ops:
  2.3 4.1 %collective-permute-start.10 = (bf16[32,2048]{1,0:T(8,128)(2,1)S(1)}, bf16[32,2048]{1,0:T(8,128)(2,1)S(1)}, u32[]{:S(2)}, u32[]{:S(2)}) collective-permute-start(bf16[32,2048]{1,0:T(8,128)(2,1)S(1)} %maximum_select_fusion), channel_id=1, source_target_pairs={{0,32},{1,33},{2,34},{3,35},{4,36},{5,37},{6,38},{7,39},{8,40},{9,... | collective-permute-start | bytes 393224 | tf_op jit(solution)/shard_map/ppermute | solution.py:52
  8.4 2.1 collective-permute-done.10
  10.5 3.3 %collective-permute-done.9 = bf16[32,2048]{1,0:T(8,128)(2,1)S(1)} collective-permute-done((bf16[32,2048]{1,0:T(8,128)(2,1)S(1)}, bf16[32,2048]{1,0:T(8,128)(2,1)S(1)}, u32[]{:S(2)}, u32[]{:S(2)}) %collective-permute-start.9) | collective-permute-done | bytes 131104 | tf_op jit(solution)/shard_map/ppermute | solution.py:52
  14.6 2.8 collective-permute-start.21
  23.6 3.1 %collective-permute-start.1 = (bf16[192,768]{1,0:T(8,128)(2,1)S(1)}, bf16[192,768]{1,0:T(8,128)(2,1)S(1)}, u32[]{:S(2)}, u32[]{:S(2)}) collective-permute-start(bf16[192,768]{1,0:T(8,128)(2,1)S(1)} %get-tuple-element.80), channel_id=1, source_target_pairs={{0,32},{16,48},{32,0},{48,16},{64,96},{80,112},{96,64},{112,80},{1... | collective-permute-start | bytes 884744 | tf_op jit(solution)/shard_map/ppermute | solution.py:57
  27.3 11.7 %collective-permute-done.21 = bf16[128,2048]{1,0:T(8,128)(2,1)} collective-permute-done((bf16[128,2048]{1,0:T(8,128)(2,1)}, bf16[128,2048]{1,0:T(8,128)(2,1)}, u32[]{:S(2)}, u32[]{:S(2)}) %collective-permute-start.21) | collective-permute-done | bytes 524320 | tf_op jit(solution)/shard_map/ppermute | solution.py:52
  39.0 1.9 constant_dynamic-update-slice_fusion.1
  40.9 2.9 %collective-permute-start.4 = (bf16[192,768]{1,0:T(8,128)(2,1)S(1)}, bf16[192,768]{1,0:T(8,128)(2,1)S(1)}, u32[]{:S(2)}, u32[]{:S(2)}) collective-permute-start(bf16[192,768]{1,0:T(8,128)(2,1)S(1)} %get-tuple-element.83), channel_id=1, source_target_pairs={{0,80},{16,64},{32,112},{48,96},{64,16},{80,0},{96,48},{112,32},{1... | collective-permute-start | bytes 884744 | tf_op jit(solution)/shard_map/ppermute | solution.py:57
  43.8 1.9 constant_dynamic-update-slice_fusion.refs_5_
  45.7 3.4 %collective-permute-start.5 = (bf16[192,768]{1,0:T(8,128)(2,1)S(1)}, bf16[192,768]{1,0:T(8,128)(2,1)S(1)}, u32[]{:S(2)}, u32[]{:S(2)}) collective-permute-start(bf16[192,768]{1,0:T(8,128)(2,1)S(1)} %get-tuple-element.84), channel_id=1, source_target_pairs={{0,96},{16,112},{32,64},{48,80},{64,32},{80,48},{96,0},{112,16},{1... | collective-permute-start | bytes 884744 | tf_op jit(solution)/shard_map/ppermute | solution.py:57
  50.3 3.0 %collective-permute-start.30 = (bf16[256,2048]{1,0:T(8,128)(2,1)}, bf16[256,2048]{1,0:T(8,128)(2,1)}, u32[]{:S(2)}, u32[]{:S(2)}) collective-permute-start(bf16[256,2048]{1,0:T(8,128)(2,1)} %constant_dynamic-update-slice_fusion.refs_5_), channel_id=1, source_target_pairs={{0,12},{1,13},{2,14},{3,15},{4,0},{5,1},{6,2},{7,3},{8,4},{9,5},{1... | collective-permute-start | bytes 3145736 | tf_op jit(solution)/shard_map/ppermute | solution.py:52
  57.7 6.3 %collective-permute-done.5.refs_6_ = bf16[192,768]{1,0:T(8,128)(2,1)S(1)} collective-permute-done((bf16[192,768]{1,0:T(8,128)(2,1)S(1)}, bf16[192,768]{1,0:T(8,128)(2,1)S(1)}, u32[]{:S(2)}, u32[]{:S(2)}) %collective-permute-start.5) | collective-permute-done | bytes 294944 | tf_op jit(solution)/shard_map/ppermute | solution.py:57
  64.0 3.3 %collective-permute-done.6.refs_7_ = bf16[192,768]{1,0:T(8,128)(2,1)S(1)} collective-permute-done((bf16[192,768]{1,0:T(8,128)(2,1)S(1)}, bf16[192,768]{1,0:T(8,128)(2,1)S(1)}, u32[]{:S(2)}, u32[]{:S(2)}) %collective-permute-start.6) | collective-permute-done | bytes 294944 | tf_op jit(solution)/shard_map/ppermute | solution.py:57
  67.3 3.1 %collective-permute-start.24 = (bf16[128,2048]{1,0:T(8,128)(2,1)}, bf16[128,2048]{1,0:T(8,128)(2,1)S(1)}, u32[]{:S(2)}, u32[]{:S(2)}) collective-permute-start(bf16[128,2048]{1,0:T(8,128)(2,1)} %pad_maximum_fusion.refs_3_), channel_id=1, source_target_pairs={{0,12},{1,13},{2,14},{3,15},{4,0},{5,1},{6,2},{7,3},{8,4},{9,5},{1... | collective-permute-start | bytes 1572872 | tf_op jit(solution)/shard_map/ppermute | solution.py:52
  70.3 5.4 %collective-permute-done.11.refs_4_ = bf16[128,2048]{1,0:T(8,128)(2,1)} collective-permute-done((bf16[128,2048]{1,0:T(8,128)(2,1)}, bf16[128,2048]{1,0:T(8,128)(2,1)}, u32[]{:S(2)}, u32[]{:S(2)}) %collective-permute-start.11) | collective-permute-done | bytes 524320 | tf_op jit(solution)/shard_map/ppermute | solution.py:52
  77.4 6.2 %collective-permute-done.24.refs_7_ = bf16[128,2048]{1,0:T(8,128)(2,1)S(1)} collective-permute-done((bf16[128,2048]{1,0:T(8,128)(2,1)}, bf16[128,2048]{1,0:T(8,128)(2,1)S(1)}, u32[]{:S(2)}, u32[]{:S(2)}) %collective-permute-start.24) | collective-permute-done | bytes 524320 | tf_op jit(solution)/shard_map/ppermute | solution.py:52
  85.1 2.8 collective-permute-start.31
  87.9 10.9 %attend.1 = (bf16[192,256]{1,0:T(8,128)(2,1)S(1)}, bf16[192,256]{1,0:T(8,128)(2,1)S(1)}, bf16[192,256]{1,0:T(8,128)(2,1)S(1)}, bf16[192,256]{1,0:T(8,128)(2,1)S(...) custom-call(bf16[192,768]{1,0:T(8,128)(2,1)S(1)} %get-tuple-element., ...), custom_call_target="tpu_custom_call" | custom-call | tf_op jit(solution)/shard_map/attend/pallas_call | solution.py:160
  103.4 3.9 %collective-permute-done.12.refs_1_ = bf16[192,256]{1,0:T(8,128)(2,1)S(1)} collective-permute-done((bf16[192,256]{1,0:T(8,128)(2,1)S(1)}, bf16[192,256]{1,0:T(8,128)(2,1)S(1)}, u32[]{:S(2)}, u32[]{:S(2)}) %collective-permute-start.12) | collective-permute-done | bytes 98336 | tf_op jit(solution)/shard_map/ppermute | solution.py:57
  107.9 3.6 %collective-permute-start.13 = (bf16[192,256]{1,0:T(8,128)(2,1)S(1)}, bf16[192,256]{1,0:T(8,128)(2,1)S(1)}, u32[]{:S(2)}, u32[]{:S(2)}) collective-permute-start(bf16[192,256]{1,0:T(8,128)(2,1)S(1)} %get-tuple-element.96.refs_10_), channel_id=1, source_target_pairs={{0,32},{16,48},{32,0},{48,16},{64,96},{80,112},{96,64},{112,80},{1... | collective-permute-start | bytes 294920 | tf_op jit(solution)/shard_map/ppermute | solution.py:57
  112.1 2.9 %grad_proj.1 = (bf16[192,2048]{1,0:T(8,128)(2,1)S(1)}, bf16[192,2048]{1,0:T(8,128)(2,1)}) custom-call(s32[2]{0:T(128)S(1)} %pad_add_fusion.ids, f32[192,4096]{1,0:T(8,128)S(1)} %bitcast.13, bf16[96,4096]{1,0:T(8,128)(2,1)S(1)} %collective-permute-done.19.refs_1_.refs_5_, f32[1,4096]{1,0:T(1,128)S(1)} %copy-done.48, f32[3,4096]{1,0:T(4,128)S(1)} %copy-done.30, ...), custom_call_target="tpu_custom_call" | custom-call | tf_op jit(solution)/shard_map/grad_proj/pallas_call | solution.py:389
  117.5 1.8 collective-permute-start.27
  119.5 12.6 %collective-permute-done.27.refs_10_ = bf16[128,2048]{1,0:T(8,128)(2,1)} collective-permute-done((bf16[128,2048]{1,0:T(8,128)(2,1)}, bf16[128,2048]{1,0:T(8,128)(2,1)}, u32[]{:S(2)}, u32[]{:S(2)}) %collective-permute-start.27) | collective-permute-done | bytes 524320 | tf_op jit(solution)/shard_map/ppermute | solution.py:52
  132.1 1.9 collective-permute-start.14
  135.4 3.9 %collective-permute-start.17 = (bf16[192,256]{1,0:T(8,128)(2,1)}, bf16[192,256]{1,0:T(8,128)(2,1)S(1)}, u32[]{:S(2)}, u32[]{:S(2)}) collective-permute-start(bf16[192,256]{1,0:T(8,128)(2,1)} %copy-done.42), channel_id=1, source_target_pairs={{0,96},{16,112},{32,64},{48,80},{64,32},{80,48},{96,0},{112,16},{1... | collective-permute-start | bytes 294920 | tf_op jit(solution)/shard_map/ppermute | solution.py:57
  146.1 8.7 %project_back.1 = (f32[8,192,256]{2,1,0:T(8,128)S(1)}, bf16[8,192,256]{2,1,0:T(8,128)(2,1)S(1)}) custom-call(s32[64]{0:T(128)S(1)} %fusion.8.refs_0_, bf16[192,2048]{1,0:T(8,128)(2,1)S(1)} %copy-done.29, bf16[192,2048]{1,0:T(8,128)(2,1)} %collective-permute-done.20.refs_2_, bf16[128,2048]{1,0:T(8,128)(2,1)} %pad_maximum_fusion.refs_3_, ...), custom_call_target="tpu_custom_call" | custom-call | tf_op jit(solution)/shard_map/project_back/pallas_call | solution.py:278
  158.3 8.2 %project.1 = (f32[192,2048]{1,0:T(8,128)S(1)}, bf16[192,2048]{1,0:T(8,128)(2,1)S(1)}) custom-call(s32[64]{0:T(128)S(1)} %fusion.8.refs_0_, bf16[8,192,256]{2,1,0:T(8,128)(2,1)S(1)} %stack.13.refs_1_, bf16[8,192,256]{2,1,0:T(8,128)(2,1)S(1)} %collective-permute-done.33.refs_2_, bf16[128,2048]{1,0:T(8,128)(2,1)} %pad_maximum_fusion.refs_3_, ...), custom_call_target="tpu_custom_call" | custom-call | tf_op jit(solution)/shard_map/project/pallas_call | solution.py:318
  166.9 2.2 collective-permute-done.34.got_ref
  169.1 2.1 mix.1
  173.5 4.8 %collective-permute-start.37 = (bf16[192,256]{1,0:T(8,128)(2,1)S(1)}, bf16[192,256]{1,0:T(8,128)(2,1)S(1)}, u32[]{:S(2)}, u32[]{:S(2)}) collective-permute-start(bf16[192,256]{1,0:T(8,128)(2,1)S(1)} %get-tuple-element.113), channel_id=1, source_target_pairs={{0,32},{16,48},{32,0},{48,16},{64,96},{80,112},{96,64},{112,80},{1... | collective-permute-start | bytes 294920 | tf_op jit(solution)/shard_map/ppermute | solution.py:57
  179.8 12.9 %collective-permute-done.36.refs_17_ = bf16[192,256]{1,0:T(8,128)(2,1)S(1)} collective-permute-done((bf16[192,256]{1,0:T(8,128)(2,1)S(1)}, bf16[192,256]{1,0:T(8,128)(2,1)S(1)}, u32[]{:S(2)}, u32[]{:S(2)}) %collective-permute-start.36) | collective-permute-done | bytes 98336 | tf_op jit(solution)/shard_map/ppermute | solution.py:57
  192.7 4.2 %collective-permute-start.40 = (bf16[192,256]{1,0:T(8,128)(2,1)S(1)}, bf16[192,256]{1,0:T(8,128)(2,1)S(1)}, u32[]{:S(2)}, u32[]{:S(2)}) collective-permute-start(bf16[192,256]{1,0:T(8,128)(2,1)S(1)} %get-tuple-element.116), channel_id=1, source_target_pairs={{0,80},{16,64},{32,112},{48,96},{64,16},{80,0},{96,48},{112,32},{1... | collective-permute-start | bytes 294920 | tf_op jit(solution)/shard_map/ppermute | solution.py:57
  200.2 5.9 %collective-permute-done.41.refs_22_ = bf16[192,256]{1,0:T(8,128)(2,1)S(1)} collective-permute-done((bf16[192,256]{1,0:T(8,128)(2,1)S(1)}, bf16[192,256]{1,0:T(8,128)(2,1)S(1)}, u32[]{:S(2)}, u32[]{:S(2)}) %collective-permute-start.41) | collective-permute-done | bytes 98336 | tf_op jit(solution)/shard_map/ppermute | solution.py:57
  207.2 8.6 %shard_map.146 = (bf16[192,384]{1,0:T(8,128)(2,1)S(1)}, bf16[192,384]{1,0:T(8,128)(2,1)S(1)}, bf16[192,384]{1,0:T(8,128)(2,1)S(1)}, bf16[192,384]{1,0:T(8,128)(2...) custom-call(bf16[192,768]{1,0:T(8,128)(2,1)S(1)} %get-tuple-element., ...), custom_call_target="tpu_custom_call" | custom-call | tf_op jit(solution)/shard_map/pallas_call | solution.py:224
  215.8 4.5 %encode.1 = (f32[192,4096]{1,0:T(8,128)}, f32[24,512]{1,0:T(8,128)S(1)}) custom-call(bf16[192,4096]{1,0:T(8,128)(2,1)S(1)} %get-tuple-element.110.mixed_ref, bf16[96,4096]{1,0:T(8,128)(2,1)S(1)} %collective-permute-done.35.prior_ref, f32[3,4096]{1,0:T(4,128)S(1)} %copy-done.31, f32[192,4096]{1,0:T(8,128)S(1)} %bitcast.15), custom_call_target="tpu_custom_call" | custom-call | tf_op jit(solution)/shard_map/encode/pallas_call | solution.py:452
  221.7 8.6 %shard_map.147 = (bf16[192,384]{1,0:T(8,128)(2,1)S(1)}, bf16[192,384]{1,0:T(8,128)(2,1)S(1)}, bf16[192,384]{1,0:T(8,128)(2,1)S(1)}, bf16[192,384]{1,0:T(8,128)(2...) custom-call(bf16[192,768]{1,0:T(8,128)(2,1)S(1)} %get-tuple-element., ...), custom_call_target="tpu_custom_call" | custom-call | tf_op jit(solution)/shard_map/pallas_call | solution.py:224
  230.4 2.5 collective-permute-start.51
  233.0 3.5 %collective-permute-start.59 = (f32[24,512]{1,0:T(8,128)S(1)}, f32[24,512]{1,0:T(8,128)S(1)}, u32[]{:S(2)}, u32[]{:S(2)}) collective-permute-start(f32[24,512]{1,0:T(8,128)S(1)} %add.106), channel_id=1, source_target_pairs={{0,8},{1,9},{2,10},{3,11},{4,12},{5,13},{6,14},{7,15},{8,0},{9,1},... | collective-permute-start | bytes 147464 | tf_op jit(solution)/shard_map/ppermute | solution.py:57
  236.5 3.3 %collective-permute-start.52 = (bf16[192,384]{1,0:T(8,128)(2,1)S(1)}, bf16[192,384]{1,0:T(8,128)(2,1)S(1)}, u32[]{:S(2)}, u32[]{:S(2)}) collective-permute-start(bf16[192,384]{1,0:T(8,128)(2,1)S(1)} %get-tuple-element.141), channel_id=1, source_target_pairs={{0,48},{16,32},{32,16},{48,0},{64,112},{80,96},{96,80},{112,64},{1... | collective-permute-start | bytes 442376 | tf_op jit(solution)/shard_map/ppermute | solution.py:57
  240.2 6.5 %collective-permute-start.60 = (f32[24,512]{1,0:T(8,128)S(1)}, f32[24,512]{1,0:T(8,128)S(1)}, u32[]{:S(2)}, u32[]{:S(2)}) collective-permute-start(f32[24,512]{1,0:T(8,128)S(1)} %add.107), channel_id=1, source_target_pairs={{0,2},{1,3},{2,0},{3,1},{4,6},{5,7},{6,4},{7,5},{8,10},{9,11},{10,... | collective-permute-start | bytes 147464 | tf_op jit(solution)/shard_map/ppermute | solution.py:57
  246.6 3.5 %collective-permute-done.60 = f32[24,512]{1,0:T(8,128)S(1)} collective-permute-done((f32[24,512]{1,0:T(8,128)S(1)}, f32[24,512]{1,0:T(8,128)S(1)}, u32[]{:S(2)}, u32[]{:S(2)}) %collective-permute-start.60) | collective-permute-done | bytes 49184 | tf_op jit(solution)/shard_map/ppermute | solution.py:57
  250.8 2.7 collective-permute-start.55
  253.5 3.8 %collective-permute-start.56 = (bf16[192,384]{1,0:T(8,128)(2,1)S(1)}, bf16[192,384]{1,0:T(8,128)(2,1)S(1)}, u32[]{:S(2)}, u32[]{:S(2)}) collective-permute-start(bf16[192,384]{1,0:T(8,128)(2,1)S(1)} %get-tuple-element.145), channel_id=1, source_target_pairs={{0,112},{16,96},{32,80},{48,64},{64,48},{80,32},{96,16},{112,0},{1... | collective-permute-start | bytes 442376 | tf_op jit(solution)/shard_map/ppermute | solution.py:57
  260.4 2.7 collective-permute-start.45
  267.4 2.0 collective-permute-start.48
  269.4 3.0 %collective-permute-start.49 = (bf16[192,384]{1,0:T(8,128)(2,1)S(1)}, bf16[192,384]{1,0:T(8,128)(2,1)S(1)}, u32[]{:S(2)}, u32[]{:S(2)}) collective-permute-start(bf16[192,384]{1,0:T(8,128)(2,1)S(1)} %get-tuple-element.137), channel_id=1, source_target_pairs={{0,112},{16,96},{32,80},{48,64},{64,48},{80,32},{96,16},{112,0},{1... | collective-permute-start | bytes 442376 | tf_op jit(solution)/shard_map/ppermute | solution.py:57
  273.9 2.3 collective-permute-done.48.refs_6_
  278.0 2.6 unpack.1
  (219 shorter events, 61.8 us)
Async XLA Ops:
  14.6 24.4 %collective-permute-start.21 = (bf16[128,2048]{1,0:T(8,128)(2,1)}, bf16[128,2048]{1,0:T(8,128)(2,1)}, u32[]{:S(2)}, u32[]{:S(2)}) collective-permute-start(bf16[128,2048]{1,0:T(8,128)(2,1)} %pad_maximum_fusion.refs_3_), channel_id=1, source_target_pairs={{0,66},{1,67},{2,64},{3,65},{4,70},{5,71},{6,68},{7,69},{8,74},{9,... | collective-permute-start | bytes 1572872 | tf_op jit(solution)/shard_map/ppermute | solution.py:52
  17.4 23.5 %collective-permute-start.22 = (bf16[128,2048]{1,0:T(8,128)(2,1)}, bf16[128,2048]{1,0:T(8,128)(2,1)}, u32[]{:S(2)}, u32[]{:S(2)}) collective-permute-start(bf16[128,2048]{1,0:T(8,128)(2,1)} %pad_maximum_fusion.refs_3_), channel_id=1, source_target_pairs={{0,2},{1,3},{2,0},{3,1},{4,6},{5,7},{6,4},{7,5},{8,10},{9,11},{10,... | collective-permute-start | bytes 1572872 | tf_op jit(solution)/shard_map/ppermute | solution.py:52
  22.6 23.1 %collective-permute-start = (bf16[192,768]{1,0:T(8,128)(2,1)S(1)}, bf16[192,768]{1,0:T(8,128)(2,1)S(1)}, u32[]{:S(2)}, u32[]{:S(2)}) collective-permute-start(bf16[192,768]{1,0:T(8,128)(2,1)S(1)} %get-tuple-element.79), channel_id=1, source_target_pairs={{0,16},{16,0},{32,48},{48,32},{64,80},{80,64},{96,112},{112,96},{1... | collective-permute-start | bytes 884744 | tf_op jit(solution)/shard_map/ppermute | solution.py:57
  23.6 25.5 %collective-permute-start.1 = (bf16[192,768]{1,0:T(8,128)(2,1)S(1)}, bf16[192,768]{1,0:T(8,128)(2,1)S(1)}, u32[]{:S(2)}, u32[]{:S(2)}) collective-permute-start(bf16[192,768]{1,0:T(8,128)(2,1)S(1)} %get-tuple-element.80), channel_id=1, source_target_pairs={{0,32},{16,48},{32,0},{48,16},{64,96},{80,112},{96,64},{112,80},{1... | collective-permute-start | bytes 884744 | tf_op jit(solution)/shard_map/ppermute | solution.py:57
  26.7 23.6 %collective-permute-start.2 = (bf16[192,768]{1,0:T(8,128)(2,1)S(1)}, bf16[192,768]{1,0:T(8,128)(2,1)S(1)}, u32[]{:S(2)}, u32[]{:S(2)}) collective-permute-start(bf16[192,768]{1,0:T(8,128)(2,1)S(1)} %get-tuple-element.81), channel_id=1, source_target_pairs={{0,48},{16,32},{32,16},{48,0},{64,112},{80,96},{96,80},{112,64},{1... | collective-permute-start | bytes 884744 | tf_op jit(solution)/shard_map/ppermute | solution.py:57
  39.0 14.4 %collective-permute-start.3 = (bf16[192,768]{1,0:T(8,128)(2,1)S(1)}, bf16[192,768]{1,0:T(8,128)(2,1)S(1)}, u32[]{:S(2)}, u32[]{:S(2)}) collective-permute-start(bf16[192,768]{1,0:T(8,128)(2,1)S(1)} %get-tuple-element.82), channel_id=1, source_target_pairs={{0,64},{16,80},{32,96},{48,112},{64,0},{80,16},{96,32},{112,48},{1... | collective-permute-start | bytes 884744 | tf_op jit(solution)/shard_map/ppermute | solution.py:57
  40.9 15.2 %collective-permute-start.4 = (bf16[192,768]{1,0:T(8,128)(2,1)S(1)}, bf16[192,768]{1,0:T(8,128)(2,1)S(1)}, u32[]{:S(2)}, u32[]{:S(2)}) collective-permute-start(bf16[192,768]{1,0:T(8,128)(2,1)S(1)} %get-tuple-element.83), channel_id=1, source_target_pairs={{0,80},{16,64},{32,112},{48,96},{64,16},{80,0},{96,48},{112,32},{1... | collective-permute-start | bytes 884744 | tf_op jit(solution)/shard_map/ppermute | solution.py:57
  45.7 18.3 %collective-permute-start.5 = (bf16[192,768]{1,0:T(8,128)(2,1)S(1)}, bf16[192,768]{1,0:T(8,128)(2,1)S(1)}, u32[]{:S(2)}, u32[]{:S(2)}) collective-permute-start(bf16[192,768]{1,0:T(8,128)(2,1)S(1)} %get-tuple-element.84), channel_id=1, source_target_pairs={{0,96},{16,112},{32,64},{48,80},{64,32},{80,48},{96,0},{112,16},{1... | collective-permute-start | bytes 884744 | tf_op jit(solution)/shard_map/ppermute | solution.py:57
  49.1 18.2 %collective-permute-start.6 = (bf16[192,768]{1,0:T(8,128)(2,1)S(1)}, bf16[192,768]{1,0:T(8,128)(2,1)S(1)}, u32[]{:S(2)}, u32[]{:S(2)}) collective-permute-start(bf16[192,768]{1,0:T(8,128)(2,1)S(1)} %get-tuple-element.85), channel_id=1, source_target_pairs={{0,112},{16,96},{32,80},{48,64},{64,48},{80,32},{96,16},{112,0},{1... | collective-permute-start | bytes 884744 | tf_op jit(solution)/shard_map/ppermute | solution.py:57
  50.3 34.8 %collective-permute-start.30 = (bf16[256,2048]{1,0:T(8,128)(2,1)}, bf16[256,2048]{1,0:T(8,128)(2,1)}, u32[]{:S(2)}, u32[]{:S(2)}) collective-permute-start(bf16[256,2048]{1,0:T(8,128)(2,1)} %constant_dynamic-update-slice_fusion.refs_5_), channel_id=1, source_target_pairs={{0,12},{1,13},{2,14},{3,15},{4,0},{5,1},{6,2},{7,3},{8,4},{9,5},{1... | collective-permute-start | bytes 3145736 | tf_op jit(solution)/shard_map/ppermute | solution.py:52
  53.5 49.2 %collective-permute-start.19 = (bf16[96,4096]{1,0:T(8,128)(2,1)S(1)}, bf16[96,4096]{1,0:T(8,128)(2,1)S(1)}, u32[]{:S(2)}, u32[]{:S(2)}) collective-permute-start(bf16[96,4096]{1,0:T(8,128)(2,1)S(1)} %fusion), channel_id=1, source_target_pairs={{16,0},{32,16},{48,32},{64,48},{80,64},{96,80},{112,96},{17,1},{33... | collective-permute-start | bytes 2359304 | tf_op jit(solution)/shard_map/ppermute | solution.py:62
  56.1 14.3 %collective-permute-start.23 = (bf16[128,2048]{1,0:T(8,128)(2,1)}, bf16[128,2048]{1,0:T(8,128)(2,1)S(1)}, u32[]{:S(2)}, u32[]{:S(2)}) collective-permute-start(bf16[128,2048]{1,0:T(8,128)(2,1)} %pad_maximum_fusion.refs_3_), channel_id=1, source_target_pairs={{0,4},{1,5},{2,6},{3,7},{4,8},{5,9},{6,10},{7,11},{8,12},{9,13},{1... | collective-permute-start | bytes 1572872 | tf_op jit(solution)/shard_map/ppermute | solution.py:52
  64.0 11.8 %collective-permute-start.11 = (bf16[128,2048]{1,0:T(8,128)(2,1)}, bf16[128,2048]{1,0:T(8,128)(2,1)}, u32[]{:S(2)}, u32[]{:S(2)}) collective-permute-start(bf16[128,2048]{1,0:T(8,128)(2,1)} %pad_maximum_fusion.refs_3_), channel_id=1, source_target_pairs={{0,64},{1,65},{2,66},{3,67},{4,68},{5,69},{6,70},{7,71},{8,72},{9,... | collective-permute-start | bytes 1572872 | tf_op jit(solution)/shard_map/ppermute | solution.py:52
  67.3 16.2 %collective-permute-start.24 = (bf16[128,2048]{1,0:T(8,128)(2,1)}, bf16[128,2048]{1,0:T(8,128)(2,1)S(1)}, u32[]{:S(2)}, u32[]{:S(2)}) collective-permute-start(bf16[128,2048]{1,0:T(8,128)(2,1)} %pad_maximum_fusion.refs_3_), channel_id=1, source_target_pairs={{0,12},{1,13},{2,14},{3,15},{4,0},{5,1},{6,2},{7,3},{8,4},{9,5},{1... | collective-permute-start | bytes 1572872 | tf_op jit(solution)/shard_map/ppermute | solution.py:52
  70.3 46.3 %collective-permute-start.25 = (bf16[128,2048]{1,0:T(8,128)(2,1)S(1)}, bf16[128,2048]{1,0:T(8,128)(2,1)S(1)}, u32[]{:S(2)}, u32[]{:S(2)}) collective-permute-start(bf16[128,2048]{1,0:T(8,128)(2,1)S(1)} %collective-permute-done.23.refs_6_), channel_id=1, source_target_pairs={{0,4},{1,5},{2,6},{3,7},{4,8},{5,9},{6,10},{7,11},{8,12},{9,13},{1... | collective-permute-start | bytes 1572872 | tf_op jit(solution)/shard_map/ppermute | solution.py:52
  75.8 43.5 %collective-permute-start.26 = (bf16[128,2048]{1,0:T(8,128)(2,1)}, bf16[128,2048]{1,0:T(8,128)(2,1)}, u32[]{:S(2)}, u32[]{:S(2)}) collective-permute-start(bf16[128,2048]{1,0:T(8,128)(2,1)} %collective-permute-done.11.refs_4_), channel_id=1, source_target_pairs={{0,4},{1,5},{2,6},{3,7},{4,8},{5,9},{6,10},{7,11},{8,12},{9,13},{1... | collective-permute-start | bytes 1572872 | tf_op jit(solution)/shard_map/ppermute | solution.py:52
  84.3 51.1 %collective-permute-start.29 = (bf16[256,2048]{1,0:T(8,128)(2,1)}, bf16[256,2048]{1,0:T(8,128)(2,1)}, u32[]{:S(2)}, u32[]{:S(2)}) collective-permute-start(bf16[256,2048]{1,0:T(8,128)(2,1)} %constant_dynamic-update-slice_fusion.refs_5_), channel_id=1, source_target_pairs={{0,4},{1,5},{2,6},{3,7},{4,8},{5,9},{6,10},{7,11},{8,12},{9,13},{1... | collective-permute-start | bytes 3145736 | tf_op jit(solution)/shard_map/ppermute | solution.py:52
  85.1 54.2 %collective-permute-start.31 = (bf16[256,2048]{1,0:T(8,128)(2,1)}, bf16[256,2048]{1,0:T(8,128)(2,1)}, u32[]{:S(2)}, u32[]{:S(2)}) collective-permute-start(bf16[256,2048]{1,0:T(8,128)(2,1)} %collective-permute-done.30.refs_13_), channel_id=1, source_target_pairs={{0,12},{1,13},{2,14},{3,15},{4,0},{5,1},{6,2},{7,3},{8,4},{9,5},{1... | collective-permute-start | bytes 3145736 | tf_op jit(solution)/shard_map/ppermute | solution.py:52
  116.6 17.4 %collective-permute-start.20 = (bf16[192,2048]{1,0:T(8,128)(2,1)}, bf16[192,2048]{1,0:T(8,128)(2,1)}, u32[]{:S(2)}, u32[]{:S(2)}) collective-permute-start(bf16[192,2048]{1,0:T(8,128)(2,1)} %get-tuple-element.103), channel_id=1, source_target_pairs={{0,1},{1,0},{2,3},{3,2},{4,5},{5,4},{6,7},{7,6},{8,9},{9,8},{10,11... | collective-permute-start | bytes 2359304 | tf_op jit(solution)/shard_map/ppermute | solution.py:52
  117.5 14.7 %collective-permute-start.27 = (bf16[128,2048]{1,0:T(8,128)(2,1)}, bf16[128,2048]{1,0:T(8,128)(2,1)}, u32[]{:S(2)}, u32[]{:S(2)}) collective-permute-start(bf16[128,2048]{1,0:T(8,128)(2,1)} %collective-permute-done.11.refs_4_), channel_id=1, source_target_pairs={{0,12},{1,13},{2,14},{3,15},{4,0},{5,1},{6,2},{7,3},{8,4},{9,5},{1... | collective-permute-start | bytes 1572872 | tf_op jit(solution)/shard_map/ppermute | solution.py:52
  119.3 15.6 %collective-permute-start.28 = (bf16[128,2048]{1,0:T(8,128)(2,1)}, bf16[128,2048]{1,0:T(8,128)(2,1)}, u32[]{:S(2)}, u32[]{:S(2)}) collective-permute-start(bf16[128,2048]{1,0:T(8,128)(2,1)} %collective-permute-done.26.refs_9_), channel_id=1, source_target_pairs={{0,4},{1,5},{2,6},{3,7},{4,8},{5,9},{6,10},{7,11},{8,12},{9,13},{1... | collective-permute-start | bytes 1572872 | tf_op jit(solution)/shard_map/ppermute | solution.py:52
  132.1 22.7 %collective-permute-start.14 = (bf16[192,256]{1,0:T(8,128)(2,1)}, bf16[192,256]{1,0:T(8,128)(2,1)S(1)}, u32[]{:S(2)}, u32[]{:S(2)}) collective-permute-start(bf16[192,256]{1,0:T(8,128)(2,1)} %copy-done.36), channel_id=1, source_target_pairs={{0,48},{16,32},{32,16},{48,0},{64,112},{80,96},{96,80},{112,64},{1... | collective-permute-start | bytes 294920 | tf_op jit(solution)/shard_map/ppermute | solution.py:57
  134.0 20.9 %collective-permute-start.15 = (bf16[192,256]{1,0:T(8,128)(2,1)}, bf16[192,256]{1,0:T(8,128)(2,1)S(1)}, u32[]{:S(2)}, u32[]{:S(2)}) collective-permute-start(bf16[192,256]{1,0:T(8,128)(2,1)} %copy-done.38), channel_id=1, source_target_pairs={{0,64},{16,80},{32,96},{48,112},{64,0},{80,16},{96,32},{112,48},{1... | collective-permute-start | bytes 294920 | tf_op jit(solution)/shard_map/ppermute | solution.py:57
  134.8 20.1 %collective-permute-start.16 = (bf16[192,256]{1,0:T(8,128)(2,1)}, bf16[192,256]{1,0:T(8,128)(2,1)S(1)}, u32[]{:S(2)}, u32[]{:S(2)}) collective-permute-start(bf16[192,256]{1,0:T(8,128)(2,1)} %copy-done.40), channel_id=1, source_target_pairs={{0,80},{16,64},{32,112},{48,96},{64,16},{80,0},{96,48},{112,32},{1... | collective-permute-start | bytes 294920 | tf_op jit(solution)/shard_map/ppermute | solution.py:57
  135.4 19.5 %collective-permute-start.17 = (bf16[192,256]{1,0:T(8,128)(2,1)}, bf16[192,256]{1,0:T(8,128)(2,1)S(1)}, u32[]{:S(2)}, u32[]{:S(2)}) collective-permute-start(bf16[192,256]{1,0:T(8,128)(2,1)} %copy-done.42), channel_id=1, source_target_pairs={{0,96},{16,112},{32,64},{48,80},{64,32},{80,48},{96,0},{112,16},{1... | collective-permute-start | bytes 294920 | tf_op jit(solution)/shard_map/ppermute | solution.py:57
  139.3 15.6 %collective-permute-start.18 = (bf16[192,256]{1,0:T(8,128)(2,1)}, bf16[192,256]{1,0:T(8,128)(2,1)S(1)}, u32[]{:S(2)}, u32[]{:S(2)}) collective-permute-start(bf16[192,256]{1,0:T(8,128)(2,1)} %copy-done.44), channel_id=1, source_target_pairs={{0,112},{16,96},{32,80},{48,64},{64,48},{80,32},{96,16},{112,0},{1... | collective-permute-start | bytes 294920 | tf_op jit(solution)/shard_map/ppermute | solution.py:57
  171.2 44.6 %collective-permute-start.35 = (bf16[96,4096]{1,0:T(8,128)(2,1)S(1)}, bf16[96,4096]{1,0:T(8,128)(2,1)S(1)}, u32[]{:S(2)}, u32[]{:S(2)}) collective-permute-start(bf16[96,4096]{1,0:T(8,128)(2,1)S(1)} %get-tuple-element.111), channel_id=1, source_target_pairs={{0,16},{16,32},{32,48},{48,64},{64,80},{80,96},{96,112},{1,17},{17... | collective-permute-start | bytes 2359304 | tf_op jit(solution)/shard_map/ppermute | solution.py:62
  172.7 20.0 %collective-permute-start.36 = (bf16[192,256]{1,0:T(8,128)(2,1)S(1)}, bf16[192,256]{1,0:T(8,128)(2,1)S(1)}, u32[]{:S(2)}, u32[]{:S(2)}) collective-permute-start(bf16[192,256]{1,0:T(8,128)(2,1)S(1)} %get-tuple-element.112), channel_id=1, source_target_pairs={{0,16},{16,0},{32,48},{48,32},{64,80},{80,64},{96,112},{112,96},{1... | collective-permute-start | bytes 294920 | tf_op jit(solution)/shard_map/ppermute | solution.py:57
  173.5 25.1 %collective-permute-start.37 = (bf16[192,256]{1,0:T(8,128)(2,1)S(1)}, bf16[192,256]{1,0:T(8,128)(2,1)S(1)}, u32[]{:S(2)}, u32[]{:S(2)}) collective-permute-start(bf16[192,256]{1,0:T(8,128)(2,1)S(1)} %get-tuple-element.113), channel_id=1, source_target_pairs={{0,32},{16,48},{32,0},{48,16},{64,96},{80,112},{96,64},{112,80},{1... | collective-permute-start | bytes 294920 | tf_op jit(solution)/shard_map/ppermute | solution.py:57
  178.3 21.9 %collective-permute-start.38 = (bf16[192,256]{1,0:T(8,128)(2,1)S(1)}, bf16[192,256]{1,0:T(8,128)(2,1)S(1)}, u32[]{:S(2)}, u32[]{:S(2)}) collective-permute-start(bf16[192,256]{1,0:T(8,128)(2,1)S(1)} %get-tuple-element.114), channel_id=1, source_target_pairs={{0,48},{16,32},{32,16},{48,0},{64,112},{80,96},{96,80},{112,64},{1... | collective-permute-start | bytes 294920 | tf_op jit(solution)/shard_map/ppermute | solution.py:57
  178.3 21.9 %collective-permute-start.39 = (bf16[192,256]{1,0:T(8,128)(2,1)S(1)}, bf16[192,256]{1,0:T(8,128)(2,1)S(1)}, u32[]{:S(2)}, u32[]{:S(2)}) collective-permute-start(bf16[192,256]{1,0:T(8,128)(2,1)S(1)} %get-tuple-element.115), channel_id=1, source_target_pairs={{0,64},{16,80},{32,96},{48,112},{64,0},{80,16},{96,32},{112,48},{1... | collective-permute-start | bytes 294920 | tf_op jit(solution)/shard_map/ppermute | solution.py:57
  221.6 11.4 %collective-permute-start.58 = (f32[24,512]{1,0:T(8,128)S(1)}, f32[24,512]{1,0:T(8,128)S(1)}, u32[]{:S(2)}, u32[]{:S(2)}) collective-permute-start(f32[24,512]{1,0:T(8,128)S(1)} %add.105), channel_id=1, source_target_pairs={{0,4},{1,5},{2,6},{3,7},{4,0},{5,1},{6,2},{7,3},{8,12},{9,13},{10,... | collective-permute-start | bytes 147464 | tf_op jit(solution)/shard_map/ppermute | solution.py:57
  230.3 20.0 %collective-permute-start.50 = (bf16[192,384]{1,0:T(8,128)(2,1)S(1)}, bf16[192,384]{1,0:T(8,128)(2,1)S(1)}, u32[]{:S(2)}, u32[]{:S(2)}) collective-permute-start(bf16[192,384]{1,0:T(8,128)(2,1)S(1)} %get-tuple-element.139), channel_id=1, source_target_pairs={{0,16},{16,0},{32,48},{48,32},{64,80},{80,64},{96,112},{112,96},{1... | collective-permute-start | bytes 442376 | tf_op jit(solution)/shard_map/ppermute | solution.py:57
  230.4 20.4 %collective-permute-start.51 = (bf16[192,384]{1,0:T(8,128)(2,1)S(1)}, bf16[192,384]{1,0:T(8,128)(2,1)S(1)}, u32[]{:S(2)}, u32[]{:S(2)}) collective-permute-start(bf16[192,384]{1,0:T(8,128)(2,1)S(1)} %get-tuple-element.140), channel_id=1, source_target_pairs={{0,32},{16,48},{32,0},{48,16},{64,96},{80,112},{96,64},{112,80},{1... | collective-permute-start | bytes 442376 | tf_op jit(solution)/shard_map/ppermute | solution.py:57
  236.5 17.0 %collective-permute-start.52 = (bf16[192,384]{1,0:T(8,128)(2,1)S(1)}, bf16[192,384]{1,0:T(8,128)(2,1)S(1)}, u32[]{:S(2)}, u32[]{:S(2)}) collective-permute-start(bf16[192,384]{1,0:T(8,128)(2,1)S(1)} %get-tuple-element.141), channel_id=1, source_target_pairs={{0,48},{16,32},{32,16},{48,0},{64,112},{80,96},{96,80},{112,64},{1... | collective-permute-start | bytes 442376 | tf_op jit(solution)/shard_map/ppermute | solution.py:57
  239.8 17.5 %collective-permute-start.53 = (bf16[192,384]{1,0:T(8,128)(2,1)S(1)}, bf16[192,384]{1,0:T(8,128)(2,1)S(1)}, u32[]{:S(2)}, u32[]{:S(2)}) collective-permute-start(bf16[192,384]{1,0:T(8,128)(2,1)S(1)} %get-tuple-element.142), channel_id=1, source_target_pairs={{0,64},{16,80},{32,96},{48,112},{64,0},{80,16},{96,32},{112,48},{1... | collective-permute-start | bytes 442376 | tf_op jit(solution)/shard_map/ppermute | solution.py:57
  240.2 10.0 %collective-permute-start.60 = (f32[24,512]{1,0:T(8,128)S(1)}, f32[24,512]{1,0:T(8,128)S(1)}, u32[]{:S(2)}, u32[]{:S(2)}) collective-permute-start(f32[24,512]{1,0:T(8,128)S(1)} %add.107), channel_id=1, source_target_pairs={{0,2},{1,3},{2,0},{3,1},{4,6},{5,7},{6,4},{7,5},{8,10},{9,11},{10,... | collective-permute-start | bytes 147464 | tf_op jit(solution)/shard_map/ppermute | solution.py:57
  250.3 8.7 %collective-permute-start.54 = (bf16[192,384]{1,0:T(8,128)(2,1)S(1)}, bf16[192,384]{1,0:T(8,128)(2,1)S(1)}, u32[]{:S(2)}, u32[]{:S(2)}) collective-permute-start(bf16[192,384]{1,0:T(8,128)(2,1)S(1)} %get-tuple-element.143), channel_id=1, source_target_pairs={{0,80},{16,64},{32,112},{48,96},{64,16},{80,0},{96,48},{112,32},{1... | collective-permute-start | bytes 442376 | tf_op jit(solution)/shard_map/ppermute | solution.py:57
  250.8 9.6 %collective-permute-start.55 = (bf16[192,384]{1,0:T(8,128)(2,1)S(1)}, bf16[192,384]{1,0:T(8,128)(2,1)S(1)}, u32[]{:S(2)}, u32[]{:S(2)}) collective-permute-start(bf16[192,384]{1,0:T(8,128)(2,1)S(1)} %get-tuple-element.144), channel_id=1, source_target_pairs={{0,96},{16,112},{32,64},{48,80},{64,32},{80,48},{96,0},{112,16},{1... | collective-permute-start | bytes 442376 | tf_op jit(solution)/shard_map/ppermute | solution.py:57
  253.5 9.6 %collective-permute-start.56 = (bf16[192,384]{1,0:T(8,128)(2,1)S(1)}, bf16[192,384]{1,0:T(8,128)(2,1)S(1)}, u32[]{:S(2)}, u32[]{:S(2)}) collective-permute-start(bf16[192,384]{1,0:T(8,128)(2,1)S(1)} %get-tuple-element.145), channel_id=1, source_target_pairs={{0,112},{16,96},{32,80},{48,64},{64,48},{80,32},{96,16},{112,0},{1... | collective-permute-start | bytes 442376 | tf_op jit(solution)/shard_map/ppermute | solution.py:57
  257.4 8.3 %collective-permute-start.43 = (bf16[192,384]{1,0:T(8,128)(2,1)S(1)}, bf16[192,384]{1,0:T(8,128)(2,1)S(1)}, u32[]{:S(2)}, u32[]{:S(2)}) collective-permute-start(bf16[192,384]{1,0:T(8,128)(2,1)S(1)} %get-tuple-element.131), channel_id=1, source_target_pairs={{0,16},{16,0},{32,48},{48,32},{64,80},{80,64},{96,112},{112,96},{1... | collective-permute-start | bytes 442376 | tf_op jit(solution)/shard_map/ppermute | solution.py:57
  257.4 10.0 %collective-permute-start.44 = (bf16[192,384]{1,0:T(8,128)(2,1)S(1)}, bf16[192,384]{1,0:T(8,128)(2,1)S(1)}, u32[]{:S(2)}, u32[]{:S(2)}) collective-permute-start(bf16[192,384]{1,0:T(8,128)(2,1)S(1)} %get-tuple-element.132), channel_id=1, source_target_pairs={{0,32},{16,48},{32,0},{48,16},{64,96},{80,112},{96,64},{112,80},{1... | collective-permute-start | bytes 442376 | tf_op jit(solution)/shard_map/ppermute | solution.py:57
  259.0 10.4 %collective-permute-start.62 = (f32[24,512]{1,0:T(8,128)S(1)}, f32[24,512]{1,0:T(8,128)S(1)}, u32[]{:S(2)}, u32[]{:S(2)}) collective-permute-start(f32[24,512]{1,0:T(8,128)S(1)} %add.109), channel_id=1, source_target_pairs={{0,16},{16,0},{32,48},{48,32},{64,80},{80,64},{96,112},{112,96},{1... | collective-permute-start | bytes 147464 | tf_op jit(solution)/shard_map/ppermute | solution.py:57
  260.4 12.0 %collective-permute-start.45 = (bf16[192,384]{1,0:T(8,128)(2,1)S(1)}, bf16[192,384]{1,0:T(8,128)(2,1)S(1)}, u32[]{:S(2)}, u32[]{:S(2)}) collective-permute-start(bf16[192,384]{1,0:T(8,128)(2,1)S(1)} %get-tuple-element.133), channel_id=1, source_target_pairs={{0,48},{16,32},{32,16},{48,0},{64,112},{80,96},{96,80},{112,64},{1... | collective-permute-start | bytes 442376 | tf_op jit(solution)/shard_map/ppermute | solution.py:57
  263.1 10.8 %collective-permute-start.46 = (bf16[192,384]{1,0:T(8,128)(2,1)S(1)}, bf16[192,384]{1,0:T(8,128)(2,1)S(1)}, u32[]{:S(2)}, u32[]{:S(2)}) collective-permute-start(bf16[192,384]{1,0:T(8,128)(2,1)S(1)} %get-tuple-element.134), channel_id=1, source_target_pairs={{0,64},{16,80},{32,96},{48,112},{64,0},{80,16},{96,32},{112,48},{1... | collective-permute-start | bytes 442376 | tf_op jit(solution)/shard_map/ppermute | solution.py:57
  265.7 8.3 %collective-permute-start.47 = (bf16[192,384]{1,0:T(8,128)(2,1)S(1)}, bf16[192,384]{1,0:T(8,128)(2,1)S(1)}, u32[]{:S(2)}, u32[]{:S(2)}) collective-permute-start(bf16[192,384]{1,0:T(8,128)(2,1)S(1)} %get-tuple-element.135), channel_id=1, source_target_pairs={{0,80},{16,64},{32,112},{48,96},{64,16},{80,0},{96,48},{112,32},{1... | collective-permute-start | bytes 442376 | tf_op jit(solution)/shard_map/ppermute | solution.py:57
  267.4 8.9 %collective-permute-start.48 = (bf16[192,384]{1,0:T(8,128)(2,1)S(1)}, bf16[192,384]{1,0:T(8,128)(2,1)S(1)}, u32[]{:S(2)}, u32[]{:S(2)}) collective-permute-start(bf16[192,384]{1,0:T(8,128)(2,1)S(1)} %get-tuple-element.136), channel_id=1, source_target_pairs={{0,96},{16,112},{32,64},{48,80},{64,32},{80,48},{96,0},{112,16},{1... | collective-permute-start | bytes 442376 | tf_op jit(solution)/shard_map/ppermute | solution.py:57
  269.4 8.7 %collective-permute-start.49 = (bf16[192,384]{1,0:T(8,128)(2,1)S(1)}, bf16[192,384]{1,0:T(8,128)(2,1)S(1)}, u32[]{:S(2)}, u32[]{:S(2)}) collective-permute-start(bf16[192,384]{1,0:T(8,128)(2,1)S(1)} %get-tuple-element.137), channel_id=1, source_target_pairs={{0,112},{16,96},{32,80},{48,64},{64,48},{80,32},{96,16},{112,0},{1... | collective-permute-start | bytes 442376 | tf_op jit(solution)/shard_map/ppermute | solution.py:57
  (71 other events, 1600.4 us)
where the time goes:
time: 282 us; the launch traced here: 281 us
  starting transfers between devices  101 us (36%)
  waiting for transfers between devices  96.5 us (34%)
  Pallas kernels  58.4 us (21%)
  local copies, waits for them, and re-layouts  22.1 us (8%)
    ppermute x42, starting transfers between devices, swap(): return lax.ppermute(array, axis, [(i, i ^ key) for i in range(count)])  73 us
    ppermute x42, waiting for transfers between devices, swap(): return lax.ppermute(array, axis, [(i, i ^ key) for i in range(count)])  49.2 us
    ppermute x20, waiting for transfers between devices, shift(): return lax.ppermute(array, AXES, pairs)  47.3 us
    ppermute x20, starting transfers between devices, shift(): return lax.ppermute(array, AXES, pairs)  25.5 us
    unnamed x111, local copies, waits for them, and re-layouts  18.5 us
    pallas_call x2, Pallas kernels, backward(): pl.pallas_call(lambda *refs: backward_body(head, *refs), in_specs=[VMEM]...  17.3 us
    pallas_call x1, Pallas kernels, forward(): pl.pallas_call(forward_body, in_specs=[VMEM] * CTX, out_specs=[VMEM] * (C...  10.9 us
    pallas_call x1, Pallas kernels, project_back(): pl.pallas_call(lambda *refs: project_back_body(runs, *refs), in_specs=[SM...  8.7 us
  transfers between devices with their start and end apart: 64, of which 26 were waited for; matrix products, arithmetic and copies ran while one was open for 2% of the time, Pallas kernels for 15%

commit v1 on v0

--- a/solution.py
+++ b/solution.py
@@ -22,6 +22,7 @@
 SPAN = (KSIZE - 1) * TOKF
 PIECE = HW // CTX
 BLOCK = 256
+WIDE = 512
 FACTOR = 1.0 / math.sqrt(HDIM)
 LOG2E = math.log2(math.e)
 AXES = ("ctx", "fsdp")
@@ -80,10 +81,11 @@
     ups, downs, out = {}, {}, list(got)
     ups[0] = shift(plane, "y", 1)
     downs[0] = shift(plane, "y", -1)
+    twice = [shift(ups[0], "y", 1)]
     for up, down in ((1, 2), (2, 1)):
         ups[up] = shift(got[up][0], "y", 1)
         downs[down] = shift(got[down][0], "y", -1)
-    twice = [shift(ups[0], "y", 1), shift(ups[1], "y", 1), shift(downs[2], "y", -1)]
+    twice += [shift(ups[1], "y", 1), shift(downs[2], "y", -1)]
     for place in range(3):
         out.append((ups[place], moved(got[place][1], "y", 1)))
         out.append((downs[place], moved(got[place][1], "y", -1)))
@@ -117,7 +119,7 @@
         in_specs=[SMEM, VMEM, VMEM, VMEM],
         out_specs=[VMEM] * CTX,
         out_shape=[shape((ROWS, 3 * PIECE), bf16)] * CTX,
-        compiler_params=params(10),
+        compiler_params=params(),
         name="pack",
     )(ids, queries, keys, values)
 
@@ -163,7 +165,7 @@
         out_specs=[VMEM] * (CTX + 1),
         out_shape=[shape((ROWS, PIECE), bf16)] * CTX + [shape((2, 8, SEQ), f32)],
         scratch_shapes=[pltpu.VMEM((2, SEQ, HDIM), bf16)] * 4,
-        compiler_params=params(24),
+        compiler_params=params(20),
         name="attend",
     )(*pieces)
 
@@ -187,17 +189,16 @@
     kt_s[...] = k_s[...].astype(f32).T.astype(bf16)
     dk_s[...] = jnp.zeros_like(dk_s)
     dv_s[...] = jnp.zeros_like(dv_s)
-    wide = 512
 
     def step(index, carry):
-        start = pl.multiple_of(index * BLOCK, BLOCK)
-        query = q_s[pl.ds(start, BLOCK), :]
-        grad = g_s[pl.ds(start, BLOCK), :]
-        delta = jnp.sum(d_s[pl.ds(start, BLOCK), :].T, axis=0, keepdims=True)
-        logs = log_ref[head, 0:1, pl.ds(start, BLOCK)]
-        dq = jnp.zeros((HDIM, BLOCK), f32)
-        for chunk in range(SEQ // wide):
-            part = slice(chunk * wide, (chunk + 1) * wide)
+        start = pl.multiple_of(index * WIDE, WIDE)
+        query = q_s[pl.ds(start, WIDE), :]
+        grad = g_s[pl.ds(start, WIDE), :]
+        delta = jnp.sum(d_s[pl.ds(start, WIDE), :].T, axis=0, keepdims=True)
+        logs = log_ref[head, 0:1, pl.ds(start, WIDE)]
+        dq = jnp.zeros((HDIM, WIDE), f32)
+        for chunk in range(SEQ // WIDE):
+            part = slice(chunk * WIDE, (chunk + 1) * WIDE)
             scores = lax.dot_general(
                 k_s[part, :], query, (((1,), (1,)), ((), ())), preferred_element_type=f32
             )
@@ -209,10 +210,10 @@
             dv_s[part, :] += jnp.dot(probs.astype(bf16), grad, preferred_element_type=f32)
             dk_s[part, :] += jnp.dot(dscore, query, preferred_element_type=f32)
             dq = dq + jnp.dot(kt_s[:, part], dscore, preferred_element_type=f32)
-        dq_s[pl.ds(start, BLOCK), :] = (dq.T * FACTOR).astype(bf16)
+        dq_s[pl.ds(start, WIDE), :] = (dq.T * FACTOR).astype(bf16)
         return carry
 
-    lax.fori_loop(0, SEQ // BLOCK, step, 0)
+    lax.fori_loop(0, SEQ // WIDE, step, 0)
     for key in range(CTX):
         rows = slice(key * ROWS, (key + 1) * ROWS)
         outs[key][:, :HDIM] = dq_s[rows, :]
@@ -515,6 +516,7 @@
         jnp.concatenate([mine, theirs], axis=0),
         jnp.concatenate([theirs, mine], axis=0),
     )
+    packed = pack(ids, queries[0], keys[0], values[0])
     gathered = gather_rows(rows)
     arrays = [g[0] for g in gathered]
     runs = []
@@ -532,7 +534,6 @@
     table = (block * PIECE + run_y * 64 + (run_x // 2) * 32).astype(jnp.int32)
     runs = [run[2:4] for run in runs]
 
-    packed = pack(ids, queries[0], keys[0], values[0])
     pieces = exchange(packed, range(1, 4))
     pieces += exchange(packed, range(4, CTX))
     later = along(cotangent[0, :SPAN].astype(bf16), -1)
@@ -557,15 +558,16 @@
     sums = add_swap(sums, "fsdp", 1)
     early = exchange_in(firsts, ((1, 4), (4, 8)))
     sums = add_swap(sums, "fsdp", 4)
-    sums = add_swap(sums, "fsdp", 8)
     seconds = backward(1, pieces, att, grads, logs)
-    sums = add_swap(after(sums, seconds[0]), "fsdp", 2)
-    late = exchange_in(seconds, ((1, 3), (3, 6), (6, 8)))
+    sums = add_swap(after(sums, seconds[0]), "fsdp", 8)
+    sums = add_swap(sums, "fsdp", 2)
+    late = exchange_in(seconds, ((1, 3), (3, 5), (5, 7), (7, 8)))
     sums = add_swap(sums, "ctx", 4)
     sums = add_swap(sums, "ctx", 1)
-    sums = add_swap(sums, "ctx", 2)
+    last = swap(sums, "ctx", 2)
+    grad_q, grad_k, grad_v = unpack(ids, early, late)
+    sums = sums + after(last, grad_q)
     grad_conv = sums.reshape(KSIZE, D)
-    grad_q, grad_k, grad_v = unpack(ids, early, late)
     return (encoded[None], grad_q[None], grad_k[None], grad_v[None], grad_conv)
 
 

time: 282 us -> 280 us (level)
  local copies, waits for them, and re-layouts: 22.1 us -> 18.7 us
    unnamed x111 -> x107, local copies, waits for them, and re-layouts: 18.5 us -> 15.1 us
  transfers between devices with their start and end apart: 64 -> 64, of which waited for: 26 -> 27; matrix products, arithmetic and copies ran while one was open for 2% -> 2% of each run, Pallas kernels for 15% -> 16%
where the time goes in v1:
time: 280 us; the launch traced here: 279 us
  starting transfers between devices  100 us (36%)
  waiting for transfers between devices  98.3 us (35%)
  Pallas kernels  58.1 us (21%)
  local copies, waits for them, and re-layouts  18.7 us (7%)
    ppermute x42, starting transfers between devices, swap(): return lax.ppermute(array, axis, [(i, i ^ key) for i in range(count)])  71.6 us
    ppermute x42, waiting for transfers between devices, swap(): return lax.ppermute(array, axis, [(i, i ^ key) for i in range(count)])  50.6 us
    ppermute x20, waiting for transfers between devices, shift(): return lax.ppermute(array, AXES, pairs)  47.7 us
    ppermute x20, starting transfers between devices, shift(): return lax.ppermute(array, AXES, pairs)  25.6 us
    unnamed x107, local copies, waits for them, and re-layouts  15.1 us
    pallas_call x2, Pallas kernels, backward(): pl.pallas_call(lambda *refs: backward_body(head, *refs), in_specs=[VMEM]...  14.5 us
    pallas_call x1, Pallas kernels, forward(): pl.pallas_call(forward_body, in_specs=[VMEM] * CTX, out_specs=[VMEM] * (C...  10.9 us
    pallas_call x1, Pallas kernels, project_back(): pl.pallas_call(lambda *refs: project_back_body(runs, *refs), in_specs=[SM...  8.7 us
  transfers between devices with their start and end apart: 64, of which 27 were waited for; matrix products, arithmetic and copies ran while one was open for 2% of the time, Pallas kernels for 16%

profile of v1, /device:TPU:0, one launch (start us, length us, event | category | flops | bytes accessed | tf_op | source)
XLA Modules:
  0.0 278.6 jit_solution(2829381100360661732)
XLA Ops:
  2.3 4.1 %collective-permute-start.10 = (bf16[32,2048]{1,0:T(8,128)(2,1)S(1)}, bf16[32,2048]{1,0:T(8,128)(2,1)S(1)}, u32[]{:S(2)}, u32[]{:S(2)}) collective-permute-start(bf16[32,2048]{1,0:T(8,128)(2,1)S(1)} %maximum_select_fusion), channel_id=1, source_target_pairs={{0,32},{1,33},{2,34},{3,35},{4,36},{5,37},{6,38},{7,39},{8,40},{9,... | collective-permute-start | bytes 393224 | tf_op jit(solution)/shard_map/ppermute | solution.py:53
  8.4 2.1 collective-permute-done.10
  10.5 3.3 %collective-permute-done.9 = bf16[32,2048]{1,0:T(8,128)(2,1)S(1)} collective-permute-done((bf16[32,2048]{1,0:T(8,128)(2,1)S(1)}, bf16[32,2048]{1,0:T(8,128)(2,1)S(1)}, u32[]{:S(2)}, u32[]{:S(2)}) %collective-permute-start.9) | collective-permute-done | bytes 131104 | tf_op jit(solution)/shard_map/ppermute | solution.py:53
  14.6 2.8 collective-permute-start.21
  18.8 3.3 %pack.1 = (bf16[192,768]{1,0:T(8,128)(2,1)}, bf16[192,768]{1,0:T(8,128)(2,1)}, bf16[192,768]{1,0:T(8,128)(2,1)}, bf16[192,768]{1,0:T(8,128)(2,1)}, bf16[192,768]...) custom-call(s32[2]{0:T(128)} %pad_add_fusion.ids, ...), custom_call_target="tpu_custom_call" | custom-call | tf_op jit(solution)/shard_map/pack/pallas_call | solution.py:117
  23.2 3.1 %collective-permute-start.1 = (bf16[192,768]{1,0:T(8,128)(2,1)}, bf16[192,768]{1,0:T(8,128)(2,1)S(1)}, u32[]{:S(2)}, u32[]{:S(2)}) collective-permute-start(bf16[192,768]{1,0:T(8,128)(2,1)} %get-tuple-element.81), channel_id=1, source_target_pairs={{0,32},{16,48},{32,0},{48,16},{64,96},{80,112},{96,64},{112,80},{1... | collective-permute-start | bytes 884744 | tf_op jit(solution)/shard_map/ppermute | solution.py:58
  26.9 12.1 %collective-permute-done.21 = bf16[128,2048]{1,0:T(8,128)(2,1)} collective-permute-done((bf16[128,2048]{1,0:T(8,128)(2,1)}, bf16[128,2048]{1,0:T(8,128)(2,1)}, u32[]{:S(2)}, u32[]{:S(2)}) %collective-permute-start.21) | collective-permute-done | bytes 524320 | tf_op jit(solution)/shard_map/ppermute | solution.py:53
  39.0 1.9 constant_dynamic-update-slice_fusion.1
  40.9 2.9 %collective-permute-start.4 = (bf16[192,768]{1,0:T(8,128)(2,1)}, bf16[192,768]{1,0:T(8,128)(2,1)S(1)}, u32[]{:S(2)}, u32[]{:S(2)}) collective-permute-start(bf16[192,768]{1,0:T(8,128)(2,1)} %get-tuple-element.84), channel_id=1, source_target_pairs={{0,80},{16,64},{32,112},{48,96},{64,16},{80,0},{96,48},{112,32},{1... | collective-permute-start | bytes 884744 | tf_op jit(solution)/shard_map/ppermute | solution.py:58
  43.8 1.9 constant_dynamic-update-slice_fusion.refs_5_
  45.7 3.4 %collective-permute-start.5 = (bf16[192,768]{1,0:T(8,128)(2,1)}, bf16[192,768]{1,0:T(8,128)(2,1)S(1)}, u32[]{:S(2)}, u32[]{:S(2)}) collective-permute-start(bf16[192,768]{1,0:T(8,128)(2,1)} %get-tuple-element.85), channel_id=1, source_target_pairs={{0,96},{16,112},{32,64},{48,80},{64,32},{80,48},{96,0},{112,16},{1... | collective-permute-start | bytes 884744 | tf_op jit(solution)/shard_map/ppermute | solution.py:58
  50.3 3.0 %collective-permute-start.30 = (bf16[256,2048]{1,0:T(8,128)(2,1)}, bf16[256,2048]{1,0:T(8,128)(2,1)}, u32[]{:S(2)}, u32[]{:S(2)}) collective-permute-start(bf16[256,2048]{1,0:T(8,128)(2,1)} %constant_dynamic-update-slice_fusion.refs_5_), channel_id=1, source_target_pairs={{0,12},{1,13},{2,14},{3,15},{4,0},{5,1},{6,2},{7,3},{8,4},{9,5},{1... | collective-permute-start | bytes 3145736 | tf_op jit(solution)/shard_map/ppermute | solution.py:53
  57.9 6.1 %collective-permute-done.5.refs_6_ = bf16[192,768]{1,0:T(8,128)(2,1)S(1)} collective-permute-done((bf16[192,768]{1,0:T(8,128)(2,1)}, bf16[192,768]{1,0:T(8,128)(2,1)S(1)}, u32[]{:S(2)}, u32[]{:S(2)}) %collective-permute-start.5) | collective-permute-done | bytes 294944 | tf_op jit(solution)/shard_map/ppermute | solution.py:58
  64.1 3.1 %collective-permute-done.6.refs_7_ = bf16[192,768]{1,0:T(8,128)(2,1)S(1)} collective-permute-done((bf16[192,768]{1,0:T(8,128)(2,1)}, bf16[192,768]{1,0:T(8,128)(2,1)S(1)}, u32[]{:S(2)}, u32[]{:S(2)}) %collective-permute-start.6) | collective-permute-done | bytes 294944 | tf_op jit(solution)/shard_map/ppermute | solution.py:58
  67.3 3.1 %collective-permute-start.24 = (bf16[128,2048]{1,0:T(8,128)(2,1)}, bf16[128,2048]{1,0:T(8,128)(2,1)S(1)}, u32[]{:S(2)}, u32[]{:S(2)}) collective-permute-start(bf16[128,2048]{1,0:T(8,128)(2,1)} %pad_maximum_fusion.refs_3_), channel_id=1, source_target_pairs={{0,12},{1,13},{2,14},{3,15},{4,0},{5,1},{6,2},{7,3},{8,4},{9,5},{1... | collective-permute-start | bytes 1572872 | tf_op jit(solution)/shard_map/ppermute | solution.py:53
  70.3 5.7 %collective-permute-done.11.refs_4_ = bf16[128,2048]{1,0:T(8,128)(2,1)} collective-permute-done((bf16[128,2048]{1,0:T(8,128)(2,1)}, bf16[128,2048]{1,0:T(8,128)(2,1)}, u32[]{:S(2)}, u32[]{:S(2)}) %collective-permute-start.11) | collective-permute-done | bytes 524320 | tf_op jit(solution)/shard_map/ppermute | solution.py:53
  77.6 5.9 %collective-permute-done.24.refs_7_ = bf16[128,2048]{1,0:T(8,128)(2,1)S(1)} collective-permute-done((bf16[128,2048]{1,0:T(8,128)(2,1)}, bf16[128,2048]{1,0:T(8,128)(2,1)S(1)}, u32[]{:S(2)}, u32[]{:S(2)}) %collective-permute-start.24) | collective-permute-done | bytes 524320 | tf_op jit(solution)/shard_map/ppermute | solution.py:53
  85.1 2.8 collective-permute-start.31
  87.9 10.9 %attend.1 = (bf16[192,256]{1,0:T(8,128)(2,1)S(1)}, bf16[192,256]{1,0:T(8,128)(2,1)S(1)}, bf16[192,256]{1,0:T(8,128)(2,1)S(1)}, bf16[192,256]{1,0:T(8,128)(2,1)S(...) custom-call(bf16[192,768]{1,0:T(8,128)(2,1)S(1)} %copy-done.2, ...), custom_call_target="tpu_custom_call" | custom-call | tf_op jit(solution)/shard_map/attend/pallas_call | solution.py:162
  103.4 3.9 %collective-permute-done.12.refs_1_ = bf16[192,256]{1,0:T(8,128)(2,1)S(1)} collective-permute-done((bf16[192,256]{1,0:T(8,128)(2,1)S(1)}, bf16[192,256]{1,0:T(8,128)(2,1)S(1)}, u32[]{:S(2)}, u32[]{:S(2)}) %collective-permute-start.12) | collective-permute-done | bytes 98336 | tf_op jit(solution)/shard_map/ppermute | solution.py:58
  108.0 3.6 %collective-permute-start.13 = (bf16[192,256]{1,0:T(8,128)(2,1)S(1)}, bf16[192,256]{1,0:T(8,128)(2,1)S(1)}, u32[]{:S(2)}, u32[]{:S(2)}) collective-permute-start(bf16[192,256]{1,0:T(8,128)(2,1)S(1)} %get-tuple-element.97.refs_10_), channel_id=1, source_target_pairs={{0,32},{16,48},{32,0},{48,16},{64,96},{80,112},{96,64},{112,80},{1... | collective-permute-start | bytes 294920 | tf_op jit(solution)/shard_map/ppermute | solution.py:58
  112.2 2.9 %grad_proj.1 = (bf16[192,2048]{1,0:T(8,128)(2,1)S(1)}, bf16[192,2048]{1,0:T(8,128)(2,1)}) custom-call(s32[2]{0:T(128)S(1)} %copy-done.51, f32[192,4096]{1,0:T(8,128)S(1)} %bitcast.13, bf16[96,4096]{1,0:T(8,128)(2,1)S(1)} %collective-permute-done.19.refs_1_.refs_5_, f32[1,4096]{1,0:T(1,128)S(1)} %copy-done.46, f32[3,4096]{1,0:T(4,128)S(1)} %copy-done.28, ...), custom_call_target="tpu_custom_call" | custom-call | tf_op jit(solution)/shard_map/grad_proj/pallas_call | solution.py:390
  119.5 12.6 %collective-permute-done.27.refs_10_ = bf16[128,2048]{1,0:T(8,128)(2,1)} collective-permute-done((bf16[128,2048]{1,0:T(8,128)(2,1)}, bf16[128,2048]{1,0:T(8,128)(2,1)}, u32[]{:S(2)}, u32[]{:S(2)}) %collective-permute-start.27) | collective-permute-done | bytes 524320 | tf_op jit(solution)/shard_map/ppermute | solution.py:53
  132.2 2.0 collective-permute-start.14
  135.4 4.0 %collective-permute-start.17 = (bf16[192,256]{1,0:T(8,128)(2,1)}, bf16[192,256]{1,0:T(8,128)(2,1)S(1)}, u32[]{:S(2)}, u32[]{:S(2)}) collective-permute-start(bf16[192,256]{1,0:T(8,128)(2,1)} %copy-done.40), channel_id=1, source_target_pairs={{0,96},{16,112},{32,64},{48,80},{64,32},{80,48},{96,0},{112,16},{1... | collective-permute-start | bytes 294920 | tf_op jit(solution)/shard_map/ppermute | solution.py:58
  146.2 8.7 %project_back.1 = (f32[8,192,256]{2,1,0:T(8,128)S(1)}, bf16[8,192,256]{2,1,0:T(8,128)(2,1)S(1)}) custom-call(s32[64]{0:T(128)S(1)} %fusion.8.refs_0_, bf16[192,2048]{1,0:T(8,128)(2,1)S(1)} %copy-done.27, bf16[192,2048]{1,0:T(8,128)(2,1)} %collective-permute-done.20.refs_2_, bf16[128,2048]{1,0:T(8,128)(2,1)} %pad_maximum_fusion.refs_3_, ...), custom_call_target="tpu_custom_call" | custom-call | tf_op jit(solution)/shard_map/project_back/pallas_call | solution.py:279
  158.4 8.2 %project.1 = (f32[192,2048]{1,0:T(8,128)S(1)}, bf16[192,2048]{1,0:T(8,128)(2,1)S(1)}) custom-call(s32[64]{0:T(128)S(1)} %fusion.8.refs_0_, bf16[8,192,256]{2,1,0:T(8,128)(2,1)S(1)} %stack.13.refs_1_, bf16[8,192,256]{2,1,0:T(8,128)(2,1)S(1)} %collective-permute-done.33.refs_2_, bf16[128,2048]{1,0:T(8,128)(2,1)} %pad_maximum_fusion.refs_3_, ...), custom_call_target="tpu_custom_call" | custom-call | tf_op jit(solution)/shard_map/project/pallas_call | solution.py:319
  167.0 2.2 collective-permute-done.34.got_ref
  169.2 2.1 mix.1
  173.5 4.9 %collective-permute-start.37 = (bf16[192,256]{1,0:T(8,128)(2,1)S(1)}, bf16[192,256]{1,0:T(8,128)(2,1)S(1)}, u32[]{:S(2)}, u32[]{:S(2)}) collective-permute-start(bf16[192,256]{1,0:T(8,128)(2,1)S(1)} %get-tuple-element.114), channel_id=1, source_target_pairs={{0,32},{16,48},{32,0},{48,16},{64,96},{80,112},{96,64},{112,80},{1... | collective-permute-start | bytes 294920 | tf_op jit(solution)/shard_map/ppermute | solution.py:58
  179.8 12.9 %collective-permute-done.36.refs_17_ = bf16[192,256]{1,0:T(8,128)(2,1)S(1)} collective-permute-done((bf16[192,256]{1,0:T(8,128)(2,1)S(1)}, bf16[192,256]{1,0:T(8,128)(2,1)S(1)}, u32[]{:S(2)}, u32[]{:S(2)}) %collective-permute-start.36) | collective-permute-done | bytes 98336 | tf_op jit(solution)/shard_map/ppermute | solution.py:58
  192.8 4.2 %collective-permute-start.40 = (bf16[192,256]{1,0:T(8,128)(2,1)S(1)}, bf16[192,256]{1,0:T(8,128)(2,1)S(1)}, u32[]{:S(2)}, u32[]{:S(2)}) collective-permute-start(bf16[192,256]{1,0:T(8,128)(2,1)S(1)} %get-tuple-element.117), channel_id=1, source_target_pairs={{0,80},{16,64},{32,112},{48,96},{64,16},{80,0},{96,48},{112,32},{1... | collective-permute-start | bytes 294920 | tf_op jit(solution)/shard_map/ppermute | solution.py:58
  200.3 5.9 %collective-permute-done.41.refs_22_ = bf16[192,256]{1,0:T(8,128)(2,1)S(1)} collective-permute-done((bf16[192,256]{1,0:T(8,128)(2,1)S(1)}, bf16[192,256]{1,0:T(8,128)(2,1)S(1)}, u32[]{:S(2)}, u32[]{:S(2)}) %collective-permute-start.41) | collective-permute-done | bytes 98336 | tf_op jit(solution)/shard_map/ppermute | solution.py:58
  207.2 7.2 %shard_map.146 = (bf16[192,384]{1,0:T(8,128)(2,1)S(1)}, bf16[192,384]{1,0:T(8,128)(2,1)S(1)}, bf16[192,384]{1,0:T(8,128)(2,1)S(1)}, bf16[192,384]{1,0:T(8,128)(2...) custom-call(bf16[192,768]{1,0:T(8,128)(2,1)S(1)} %copy-done.2, ...), custom_call_target="tpu_custom_call" | custom-call | tf_op jit(solution)/shard_map/pallas_call | solution.py:225
  214.5 4.5 %encode.1 = (f32[192,4096]{1,0:T(8,128)}, f32[24,512]{1,0:T(8,128)S(1)}) custom-call(bf16[192,4096]{1,0:T(8,128)(2,1)S(1)} %get-tuple-element.111.mixed_ref, bf16[96,4096]{1,0:T(8,128)(2,1)S(1)} %collective-permute-done.35.prior_ref, f32[3,4096]{1,0:T(4,128)S(1)} %copy-done.29, f32[192,4096]{1,0:T(8,128)S(1)} %bitcast.15), custom_call_target="tpu_custom_call" | custom-call | tf_op jit(solution)/shard_map/encode/pallas_call | solution.py:453
  220.5 7.2 %shard_map.147 = (bf16[192,384]{1,0:T(8,128)(2,1)S(1)}, bf16[192,384]{1,0:T(8,128)(2,1)S(1)}, bf16[192,384]{1,0:T(8,128)(2,1)S(1)}, bf16[192,384]{1,0:T(8,128)(2...) custom-call(bf16[192,768]{1,0:T(8,128)(2,1)S(1)} %copy-done.2, ...), custom_call_target="tpu_custom_call" | custom-call | tf_op jit(solution)/shard_map/pallas_call | solution.py:225
  227.9 2.6 collective-permute-start.51
  230.5 2.1 collective-permute-start.52
  232.6 4.5 %collective-permute-start.59 = (f32[24,512]{1,0:T(8,128)S(1)}, f32[24,512]{1,0:T(8,128)S(1)}, u32[]{:S(2)}, u32[]{:S(2)}) collective-permute-start(f32[24,512]{1,0:T(8,128)S(1)} %add.106), channel_id=1, source_target_pairs={{0,8},{1,9},{2,10},{3,11},{4,12},{5,13},{6,14},{7,15},{8,0},{9,1},... | collective-permute-start | bytes 147464 | tf_op jit(solution)/shard_map/ppermute | solution.py:58
  239.2 4.8 %collective-permute-start.60 = (f32[24,512]{1,0:T(8,128)S(1)}, f32[24,512]{1,0:T(8,128)S(1)}, u32[]{:S(2)}, u32[]{:S(2)}) collective-permute-start(f32[24,512]{1,0:T(8,128)S(1)} %add.107), channel_id=1, source_target_pairs={{0,2},{1,3},{2,0},{3,1},{4,6},{5,7},{6,4},{7,5},{8,10},{9,11},{10,... | collective-permute-start | bytes 147464 | tf_op jit(solution)/shard_map/ppermute | solution.py:58
  244.0 3.4 %collective-permute-done.60 = f32[24,512]{1,0:T(8,128)S(1)} collective-permute-done((f32[24,512]{1,0:T(8,128)S(1)}, f32[24,512]{1,0:T(8,128)S(1)}, u32[]{:S(2)}, u32[]{:S(2)}) %collective-permute-start.60) | collective-permute-done | bytes 49184 | tf_op jit(solution)/shard_map/ppermute | solution.py:58
  248.1 2.7 collective-permute-start.55
  250.8 3.8 %collective-permute-start.56 = (bf16[192,384]{1,0:T(8,128)(2,1)S(1)}, bf16[192,384]{1,0:T(8,128)(2,1)S(1)}, u32[]{:S(2)}, u32[]{:S(2)}) collective-permute-start(bf16[192,384]{1,0:T(8,128)(2,1)S(1)} %get-tuple-element.146), channel_id=1, source_target_pairs={{0,112},{16,96},{32,80},{48,64},{64,48},{80,32},{96,16},{112,0},{1... | collective-permute-start | bytes 442376 | tf_op jit(solution)/shard_map/ppermute | solution.py:58
  257.7 2.7 collective-permute-start.45
  264.7 2.0 collective-permute-start.48
  266.7 3.0 %collective-permute-start.49 = (bf16[192,384]{1,0:T(8,128)(2,1)S(1)}, bf16[192,384]{1,0:T(8,128)(2,1)S(1)}, u32[]{:S(2)}, u32[]{:S(2)}) collective-permute-start(bf16[192,384]{1,0:T(8,128)(2,1)S(1)} %get-tuple-element.138), channel_id=1, source_target_pairs={{0,112},{16,96},{32,80},{48,64},{64,48},{80,32},{96,16},{112,0},{1... | collective-permute-start | bytes 442376 | tf_op jit(solution)/shard_map/ppermute | solution.py:58
  271.2 2.3 collective-permute-done.48.refs_6_
  275.3 2.6 unpack.1
  (215 shorter events, 62.1 us)
Async XLA Ops:
  14.6 24.4 %collective-permute-start.21 = (bf16[128,2048]{1,0:T(8,128)(2,1)}, bf16[128,2048]{1,0:T(8,128)(2,1)}, u32[]{:S(2)}, u32[]{:S(2)}) collective-permute-start(bf16[128,2048]{1,0:T(8,128)(2,1)} %pad_maximum_fusion.refs_3_), channel_id=1, source_target_pairs={{0,66},{1,67},{2,64},{3,65},{4,70},{5,71},{6,68},{7,69},{8,74},{9,... | collective-permute-start | bytes 1572872 | tf_op jit(solution)/shard_map/ppermute | solution.py:53
  17.4 23.5 %collective-permute-start.22 = (bf16[128,2048]{1,0:T(8,128)(2,1)}, bf16[128,2048]{1,0:T(8,128)(2,1)}, u32[]{:S(2)}, u32[]{:S(2)}) collective-permute-start(bf16[128,2048]{1,0:T(8,128)(2,1)} %pad_maximum_fusion.refs_3_), channel_id=1, source_target_pairs={{0,2},{1,3},{2,0},{3,1},{4,6},{5,7},{6,4},{7,5},{8,10},{9,11},{10,... | collective-permute-start | bytes 1572872 | tf_op jit(solution)/shard_map/ppermute | solution.py:53
  22.2 23.5 %collective-permute-start = (bf16[192,768]{1,0:T(8,128)(2,1)}, bf16[192,768]{1,0:T(8,128)(2,1)S(1)}, u32[]{:S(2)}, u32[]{:S(2)}) collective-permute-start(bf16[192,768]{1,0:T(8,128)(2,1)} %get-tuple-element.80), channel_id=1, source_target_pairs={{0,16},{16,0},{32,48},{48,32},{64,80},{80,64},{96,112},{112,96},{1... | collective-permute-start | bytes 884744 | tf_op jit(solution)/shard_map/ppermute | solution.py:58
  23.2 25.9 %collective-permute-start.1 = (bf16[192,768]{1,0:T(8,128)(2,1)}, bf16[192,768]{1,0:T(8,128)(2,1)S(1)}, u32[]{:S(2)}, u32[]{:S(2)}) collective-permute-start(bf16[192,768]{1,0:T(8,128)(2,1)} %get-tuple-element.81), channel_id=1, source_target_pairs={{0,32},{16,48},{32,0},{48,16},{64,96},{80,112},{96,64},{112,80},{1... | collective-permute-start | bytes 884744 | tf_op jit(solution)/shard_map/ppermute | solution.py:58
  26.3 24.0 %collective-permute-start.2 = (bf16[192,768]{1,0:T(8,128)(2,1)}, bf16[192,768]{1,0:T(8,128)(2,1)S(1)}, u32[]{:S(2)}, u32[]{:S(2)}) collective-permute-start(bf16[192,768]{1,0:T(8,128)(2,1)} %get-tuple-element.82), channel_id=1, source_target_pairs={{0,48},{16,32},{32,16},{48,0},{64,112},{80,96},{96,80},{112,64},{1... | collective-permute-start | bytes 884744 | tf_op jit(solution)/shard_map/ppermute | solution.py:58
  39.0 14.4 %collective-permute-start.3 = (bf16[192,768]{1,0:T(8,128)(2,1)}, bf16[192,768]{1,0:T(8,128)(2,1)S(1)}, u32[]{:S(2)}, u32[]{:S(2)}) collective-permute-start(bf16[192,768]{1,0:T(8,128)(2,1)} %get-tuple-element.83), channel_id=1, source_target_pairs={{0,64},{16,80},{32,96},{48,112},{64,0},{80,16},{96,32},{112,48},{1... | collective-permute-start | bytes 884744 | tf_op jit(solution)/shard_map/ppermute | solution.py:58
  40.9 15.4 %collective-permute-start.4 = (bf16[192,768]{1,0:T(8,128)(2,1)}, bf16[192,768]{1,0:T(8,128)(2,1)S(1)}, u32[]{:S(2)}, u32[]{:S(2)}) collective-permute-start(bf16[192,768]{1,0:T(8,128)(2,1)} %get-tuple-element.84), channel_id=1, source_target_pairs={{0,80},{16,64},{32,112},{48,96},{64,16},{80,0},{96,48},{112,32},{1... | collective-permute-start | bytes 884744 | tf_op jit(solution)/shard_map/ppermute | solution.py:58
  45.7 18.3 %collective-permute-start.5 = (bf16[192,768]{1,0:T(8,128)(2,1)}, bf16[192,768]{1,0:T(8,128)(2,1)S(1)}, u32[]{:S(2)}, u32[]{:S(2)}) collective-permute-start(bf16[192,768]{1,0:T(8,128)(2,1)} %get-tuple-element.85), channel_id=1, source_target_pairs={{0,96},{16,112},{32,64},{48,80},{64,32},{80,48},{96,0},{112,16},{1... | collective-permute-start | bytes 884744 | tf_op jit(solution)/shard_map/ppermute | solution.py:58
  49.1 18.2 %collective-permute-start.6 = (bf16[192,768]{1,0:T(8,128)(2,1)}, bf16[192,768]{1,0:T(8,128)(2,1)S(1)}, u32[]{:S(2)}, u32[]{:S(2)}) collective-permute-start(bf16[192,768]{1,0:T(8,128)(2,1)} %get-tuple-element.86), channel_id=1, source_target_pairs={{0,112},{16,96},{32,80},{48,64},{64,48},{80,32},{96,16},{112,0},{1... | collective-permute-start | bytes 884744 | tf_op jit(solution)/shard_map/ppermute | solution.py:58
  50.3 34.8 %collective-permute-start.30 = (bf16[256,2048]{1,0:T(8,128)(2,1)}, bf16[256,2048]{1,0:T(8,128)(2,1)}, u32[]{:S(2)}, u32[]{:S(2)}) collective-permute-start(bf16[256,2048]{1,0:T(8,128)(2,1)} %constant_dynamic-update-slice_fusion.refs_5_), channel_id=1, source_target_pairs={{0,12},{1,13},{2,14},{3,15},{4,0},{5,1},{6,2},{7,3},{8,4},{9,5},{1... | collective-permute-start | bytes 3145736 | tf_op jit(solution)/shard_map/ppermute | solution.py:53
  53.5 49.2 %collective-permute-start.19 = (bf16[96,4096]{1,0:T(8,128)(2,1)S(1)}, bf16[96,4096]{1,0:T(8,128)(2,1)S(1)}, u32[]{:S(2)}, u32[]{:S(2)}) collective-permute-start(bf16[96,4096]{1,0:T(8,128)(2,1)S(1)} %fusion), channel_id=1, source_target_pairs={{16,0},{32,16},{48,32},{64,48},{80,64},{96,80},{112,96},{17,1},{33... | collective-permute-start | bytes 2359304 | tf_op jit(solution)/shard_map/ppermute | solution.py:63
  56.2 14.1 %collective-permute-start.23 = (bf16[128,2048]{1,0:T(8,128)(2,1)}, bf16[128,2048]{1,0:T(8,128)(2,1)S(1)}, u32[]{:S(2)}, u32[]{:S(2)}) collective-permute-start(bf16[128,2048]{1,0:T(8,128)(2,1)} %pad_maximum_fusion.refs_3_), channel_id=1, source_target_pairs={{0,4},{1,5},{2,6},{3,7},{4,8},{5,9},{6,10},{7,11},{8,12},{9,13},{1... | collective-permute-start | bytes 1572872 | tf_op jit(solution)/shard_map/ppermute | solution.py:53
  64.0 12.0 %collective-permute-start.11 = (bf16[128,2048]{1,0:T(8,128)(2,1)}, bf16[128,2048]{1,0:T(8,128)(2,1)}, u32[]{:S(2)}, u32[]{:S(2)}) collective-permute-start(bf16[128,2048]{1,0:T(8,128)(2,1)} %pad_maximum_fusion.refs_3_), channel_id=1, source_target_pairs={{0,64},{1,65},{2,66},{3,67},{4,68},{5,69},{6,70},{7,71},{8,72},{9,... | collective-permute-start | bytes 1572872 | tf_op jit(solution)/shard_map/ppermute | solution.py:53
  67.3 16.2 %collective-permute-start.24 = (bf16[128,2048]{1,0:T(8,128)(2,1)}, bf16[128,2048]{1,0:T(8,128)(2,1)S(1)}, u32[]{:S(2)}, u32[]{:S(2)}) collective-permute-start(bf16[128,2048]{1,0:T(8,128)(2,1)} %pad_maximum_fusion.refs_3_), channel_id=1, source_target_pairs={{0,12},{1,13},{2,14},{3,15},{4,0},{5,1},{6,2},{7,3},{8,4},{9,5},{1... | collective-permute-start | bytes 1572872 | tf_op jit(solution)/shard_map/ppermute | solution.py:53
  70.3 46.4 %collective-permute-start.25 = (bf16[128,2048]{1,0:T(8,128)(2,1)S(1)}, bf16[128,2048]{1,0:T(8,128)(2,1)S(1)}, u32[]{:S(2)}, u32[]{:S(2)}) collective-permute-start(bf16[128,2048]{1,0:T(8,128)(2,1)S(1)} %collective-permute-done.23.refs_6_), channel_id=1, source_target_pairs={{0,4},{1,5},{2,6},{3,7},{4,8},{5,9},{6,10},{7,11},{8,12},{9,13},{1... | collective-permute-start | bytes 1572872 | tf_op jit(solution)/shard_map/ppermute | solution.py:53
  76.0 43.3 %collective-permute-start.26 = (bf16[128,2048]{1,0:T(8,128)(2,1)}, bf16[128,2048]{1,0:T(8,128)(2,1)}, u32[]{:S(2)}, u32[]{:S(2)}) collective-permute-start(bf16[128,2048]{1,0:T(8,128)(2,1)} %collective-permute-done.11.refs_4_), channel_id=1, source_target_pairs={{0,4},{1,5},{2,6},{3,7},{4,8},{5,9},{6,10},{7,11},{8,12},{9,13},{1... | collective-permute-start | bytes 1572872 | tf_op jit(solution)/shard_map/ppermute | solution.py:53
  84.3 51.1 %collective-permute-start.29 = (bf16[256,2048]{1,0:T(8,128)(2,1)}, bf16[256,2048]{1,0:T(8,128)(2,1)}, u32[]{:S(2)}, u32[]{:S(2)}) collective-permute-start(bf16[256,2048]{1,0:T(8,128)(2,1)} %constant_dynamic-update-slice_fusion.refs_5_), channel_id=1, source_target_pairs={{0,4},{1,5},{2,6},{3,7},{4,8},{5,9},{6,10},{7,11},{8,12},{9,13},{1... | collective-permute-start | bytes 3145736 | tf_op jit(solution)/shard_map/ppermute | solution.py:53
  85.1 54.3 %collective-permute-start.31 = (bf16[256,2048]{1,0:T(8,128)(2,1)}, bf16[256,2048]{1,0:T(8,128)(2,1)}, u32[]{:S(2)}, u32[]{:S(2)}) collective-permute-start(bf16[256,2048]{1,0:T(8,128)(2,1)} %collective-permute-done.30.refs_13_), channel_id=1, source_target_pairs={{0,12},{1,13},{2,14},{3,15},{4,0},{5,1},{6,2},{7,3},{8,4},{9,5},{1... | collective-permute-start | bytes 3145736 | tf_op jit(solution)/shard_map/ppermute | solution.py:53
  116.7 17.4 %collective-permute-start.20 = (bf16[192,2048]{1,0:T(8,128)(2,1)}, bf16[192,2048]{1,0:T(8,128)(2,1)}, u32[]{:S(2)}, u32[]{:S(2)}) collective-permute-start(bf16[192,2048]{1,0:T(8,128)(2,1)} %get-tuple-element.104), channel_id=1, source_target_pairs={{0,1},{1,0},{2,3},{3,2},{4,5},{5,4},{6,7},{7,6},{8,9},{9,8},{10,11... | collective-permute-start | bytes 2359304 | tf_op jit(solution)/shard_map/ppermute | solution.py:53
  117.5 14.7 %collective-permute-start.27 = (bf16[128,2048]{1,0:T(8,128)(2,1)}, bf16[128,2048]{1,0:T(8,128)(2,1)}, u32[]{:S(2)}, u32[]{:S(2)}) collective-permute-start(bf16[128,2048]{1,0:T(8,128)(2,1)} %collective-permute-done.11.refs_4_), channel_id=1, source_target_pairs={{0,12},{1,13},{2,14},{3,15},{4,0},{5,1},{6,2},{7,3},{8,4},{9,5},{1... | collective-permute-start | bytes 1572872 | tf_op jit(solution)/shard_map/ppermute | solution.py:53
  119.3 15.6 %collective-permute-start.28 = (bf16[128,2048]{1,0:T(8,128)(2,1)}, bf16[128,2048]{1,0:T(8,128)(2,1)}, u32[]{:S(2)}, u32[]{:S(2)}) collective-permute-start(bf16[128,2048]{1,0:T(8,128)(2,1)} %collective-permute-done.26.refs_9_), channel_id=1, source_target_pairs={{0,4},{1,5},{2,6},{3,7},{4,8},{5,9},{6,10},{7,11},{8,12},{9,13},{1... | collective-permute-start | bytes 1572872 | tf_op jit(solution)/shard_map/ppermute | solution.py:53
  132.2 22.8 %collective-permute-start.14 = (bf16[192,256]{1,0:T(8,128)(2,1)}, bf16[192,256]{1,0:T(8,128)(2,1)S(1)}, u32[]{:S(2)}, u32[]{:S(2)}) collective-permute-start(bf16[192,256]{1,0:T(8,128)(2,1)} %copy-done.34), channel_id=1, source_target_pairs={{0,48},{16,32},{32,16},{48,0},{64,112},{80,96},{96,80},{112,64},{1... | collective-permute-start | bytes 294920 | tf_op jit(solution)/shard_map/ppermute | solution.py:58
  134.1 20.9 %collective-permute-start.15 = (bf16[192,256]{1,0:T(8,128)(2,1)}, bf16[192,256]{1,0:T(8,128)(2,1)S(1)}, u32[]{:S(2)}, u32[]{:S(2)}) collective-permute-start(bf16[192,256]{1,0:T(8,128)(2,1)} %copy-done.36), channel_id=1, source_target_pairs={{0,64},{16,80},{32,96},{48,112},{64,0},{80,16},{96,32},{112,48},{1... | collective-permute-start | bytes 294920 | tf_op jit(solution)/shard_map/ppermute | solution.py:58
  134.9 20.1 %collective-permute-start.16 = (bf16[192,256]{1,0:T(8,128)(2,1)}, bf16[192,256]{1,0:T(8,128)(2,1)S(1)}, u32[]{:S(2)}, u32[]{:S(2)}) collective-permute-start(bf16[192,256]{1,0:T(8,128)(2,1)} %copy-done.38), channel_id=1, source_target_pairs={{0,80},{16,64},{32,112},{48,96},{64,16},{80,0},{96,48},{112,32},{1... | collective-permute-start | bytes 294920 | tf_op jit(solution)/shard_map/ppermute | solution.py:58
  135.4 19.6 %collective-permute-start.17 = (bf16[192,256]{1,0:T(8,128)(2,1)}, bf16[192,256]{1,0:T(8,128)(2,1)S(1)}, u32[]{:S(2)}, u32[]{:S(2)}) collective-permute-start(bf16[192,256]{1,0:T(8,128)(2,1)} %copy-done.40), channel_id=1, source_target_pairs={{0,96},{16,112},{32,64},{48,80},{64,32},{80,48},{96,0},{112,16},{1... | collective-permute-start | bytes 294920 | tf_op jit(solution)/shard_map/ppermute | solution.py:58
  139.4 15.6 %collective-permute-start.18 = (bf16[192,256]{1,0:T(8,128)(2,1)}, bf16[192,256]{1,0:T(8,128)(2,1)S(1)}, u32[]{:S(2)}, u32[]{:S(2)}) collective-permute-start(bf16[192,256]{1,0:T(8,128)(2,1)} %copy-done.42), channel_id=1, source_target_pairs={{0,112},{16,96},{32,80},{48,64},{64,48},{80,32},{96,16},{112,0},{1... | collective-permute-start | bytes 294920 | tf_op jit(solution)/shard_map/ppermute | solution.py:58
  171.3 43.1 %collective-permute-start.35 = (bf16[96,4096]{1,0:T(8,128)(2,1)S(1)}, bf16[96,4096]{1,0:T(8,128)(2,1)S(1)}, u32[]{:S(2)}, u32[]{:S(2)}) collective-permute-start(bf16[96,4096]{1,0:T(8,128)(2,1)S(1)} %get-tuple-element.112), channel_id=1, source_target_pairs={{0,16},{16,32},{32,48},{48,64},{64,80},{80,96},{96,112},{1,17},{17... | collective-permute-start | bytes 2359304 | tf_op jit(solution)/shard_map/ppermute | solution.py:63
  172.8 20.0 %collective-permute-start.36 = (bf16[192,256]{1,0:T(8,128)(2,1)S(1)}, bf16[192,256]{1,0:T(8,128)(2,1)S(1)}, u32[]{:S(2)}, u32[]{:S(2)}) collective-permute-start(bf16[192,256]{1,0:T(8,128)(2,1)S(1)} %get-tuple-element.113), channel_id=1, source_target_pairs={{0,16},{16,0},{32,48},{48,32},{64,80},{80,64},{96,112},{112,96},{1... | collective-permute-start | bytes 294920 | tf_op jit(solution)/shard_map/ppermute | solution.py:58
  173.5 25.1 %collective-permute-start.37 = (bf16[192,256]{1,0:T(8,128)(2,1)S(1)}, bf16[192,256]{1,0:T(8,128)(2,1)S(1)}, u32[]{:S(2)}, u32[]{:S(2)}) collective-permute-start(bf16[192,256]{1,0:T(8,128)(2,1)S(1)} %get-tuple-element.114), channel_id=1, source_target_pairs={{0,32},{16,48},{32,0},{48,16},{64,96},{80,112},{96,64},{112,80},{1... | collective-permute-start | bytes 294920 | tf_op jit(solution)/shard_map/ppermute | solution.py:58
  178.3 21.9 %collective-permute-start.38 = (bf16[192,256]{1,0:T(8,128)(2,1)S(1)}, bf16[192,256]{1,0:T(8,128)(2,1)S(1)}, u32[]{:S(2)}, u32[]{:S(2)}) collective-permute-start(bf16[192,256]{1,0:T(8,128)(2,1)S(1)} %get-tuple-element.115), channel_id=1, source_target_pairs={{0,48},{16,32},{32,16},{48,0},{64,112},{80,96},{96,80},{112,64},{1... | collective-permute-start | bytes 294920 | tf_op jit(solution)/shard_map/ppermute | solution.py:58
  178.4 21.9 %collective-permute-start.39 = (bf16[192,256]{1,0:T(8,128)(2,1)S(1)}, bf16[192,256]{1,0:T(8,128)(2,1)S(1)}, u32[]{:S(2)}, u32[]{:S(2)}) collective-permute-start(bf16[192,256]{1,0:T(8,128)(2,1)S(1)} %get-tuple-element.116), channel_id=1, source_target_pairs={{0,64},{16,80},{32,96},{48,112},{64,0},{80,16},{96,32},{112,48},{1... | collective-permute-start | bytes 294920 | tf_op jit(solution)/shard_map/ppermute | solution.py:58
  220.2 12.3 %collective-permute-start.58 = (f32[24,512]{1,0:T(8,128)S(1)}, f32[24,512]{1,0:T(8,128)S(1)}, u32[]{:S(2)}, u32[]{:S(2)}) collective-permute-start(f32[24,512]{1,0:T(8,128)S(1)} %add.105), channel_id=1, source_target_pairs={{0,4},{1,5},{2,6},{3,7},{4,0},{5,1},{6,2},{7,3},{8,12},{9,13},{10,... | collective-permute-start | bytes 147464 | tf_op jit(solution)/shard_map/ppermute | solution.py:58
  227.8 19.8 %collective-permute-start.50 = (bf16[192,384]{1,0:T(8,128)(2,1)S(1)}, bf16[192,384]{1,0:T(8,128)(2,1)S(1)}, u32[]{:S(2)}, u32[]{:S(2)}) collective-permute-start(bf16[192,384]{1,0:T(8,128)(2,1)S(1)} %get-tuple-element.140), channel_id=1, source_target_pairs={{0,16},{16,0},{32,48},{48,32},{64,80},{80,64},{96,112},{112,96},{1... | collective-permute-start | bytes 442376 | tf_op jit(solution)/shard_map/ppermute | solution.py:58
  227.9 20.2 %collective-permute-start.51 = (bf16[192,384]{1,0:T(8,128)(2,1)S(1)}, bf16[192,384]{1,0:T(8,128)(2,1)S(1)}, u32[]{:S(2)}, u32[]{:S(2)}) collective-permute-start(bf16[192,384]{1,0:T(8,128)(2,1)S(1)} %get-tuple-element.141), channel_id=1, source_target_pairs={{0,32},{16,48},{32,0},{48,16},{64,96},{80,112},{96,64},{112,80},{1... | collective-permute-start | bytes 442376 | tf_op jit(solution)/shard_map/ppermute | solution.py:58
  230.5 20.3 %collective-permute-start.52 = (bf16[192,384]{1,0:T(8,128)(2,1)S(1)}, bf16[192,384]{1,0:T(8,128)(2,1)S(1)}, u32[]{:S(2)}, u32[]{:S(2)}) collective-permute-start(bf16[192,384]{1,0:T(8,128)(2,1)S(1)} %get-tuple-element.142), channel_id=1, source_target_pairs={{0,48},{16,32},{32,16},{48,0},{64,112},{80,96},{96,80},{112,64},{1... | collective-permute-start | bytes 442376 | tf_op jit(solution)/shard_map/ppermute | solution.py:58
  237.1 17.5 %collective-permute-start.53 = (bf16[192,384]{1,0:T(8,128)(2,1)S(1)}, bf16[192,384]{1,0:T(8,128)(2,1)S(1)}, u32[]{:S(2)}, u32[]{:S(2)}) collective-permute-start(bf16[192,384]{1,0:T(8,128)(2,1)S(1)} %get-tuple-element.143), channel_id=1, source_target_pairs={{0,64},{16,80},{32,96},{48,112},{64,0},{80,16},{96,32},{112,48},{1... | collective-permute-start | bytes 442376 | tf_op jit(solution)/shard_map/ppermute | solution.py:58
  239.2 8.3 %collective-permute-start.60 = (f32[24,512]{1,0:T(8,128)S(1)}, f32[24,512]{1,0:T(8,128)S(1)}, u32[]{:S(2)}, u32[]{:S(2)}) collective-permute-start(f32[24,512]{1,0:T(8,128)S(1)} %add.107), channel_id=1, source_target_pairs={{0,2},{1,3},{2,0},{3,1},{4,6},{5,7},{6,4},{7,5},{8,10},{9,11},{10,... | collective-permute-start | bytes 147464 | tf_op jit(solution)/shard_map/ppermute | solution.py:58
  247.6 8.7 %collective-permute-start.54 = (bf16[192,384]{1,0:T(8,128)(2,1)S(1)}, bf16[192,384]{1,0:T(8,128)(2,1)S(1)}, u32[]{:S(2)}, u32[]{:S(2)}) collective-permute-start(bf16[192,384]{1,0:T(8,128)(2,1)S(1)} %get-tuple-element.144), channel_id=1, source_target_pairs={{0,80},{16,64},{32,112},{48,96},{64,16},{80,0},{96,48},{112,32},{1... | collective-permute-start | bytes 442376 | tf_op jit(solution)/shard_map/ppermute | solution.py:58
  248.1 9.6 %collective-permute-start.55 = (bf16[192,384]{1,0:T(8,128)(2,1)S(1)}, bf16[192,384]{1,0:T(8,128)(2,1)S(1)}, u32[]{:S(2)}, u32[]{:S(2)}) collective-permute-start(bf16[192,384]{1,0:T(8,128)(2,1)S(1)} %get-tuple-element.145), channel_id=1, source_target_pairs={{0,96},{16,112},{32,64},{48,80},{64,32},{80,48},{96,0},{112,16},{1... | collective-permute-start | bytes 442376 | tf_op jit(solution)/shard_map/ppermute | solution.py:58
  250.8 9.6 %collective-permute-start.56 = (bf16[192,384]{1,0:T(8,128)(2,1)S(1)}, bf16[192,384]{1,0:T(8,128)(2,1)S(1)}, u32[]{:S(2)}, u32[]{:S(2)}) collective-permute-start(bf16[192,384]{1,0:T(8,128)(2,1)S(1)} %get-tuple-element.146), channel_id=1, source_target_pairs={{0,112},{16,96},{32,80},{48,64},{64,48},{80,32},{96,16},{112,0},{1... | collective-permute-start | bytes 442376 | tf_op jit(solution)/shard_map/ppermute | solution.py:58
  254.6 8.3 %collective-permute-start.43 = (bf16[192,384]{1,0:T(8,128)(2,1)S(1)}, bf16[192,384]{1,0:T(8,128)(2,1)S(1)}, u32[]{:S(2)}, u32[]{:S(2)}) collective-permute-start(bf16[192,384]{1,0:T(8,128)(2,1)S(1)} %get-tuple-element.132), channel_id=1, source_target_pairs={{0,16},{16,0},{32,48},{48,32},{64,80},{80,64},{96,112},{112,96},{1... | collective-permute-start | bytes 442376 | tf_op jit(solution)/shard_map/ppermute | solution.py:58
  254.6 10.0 %collective-permute-start.44 = (bf16[192,384]{1,0:T(8,128)(2,1)S(1)}, bf16[192,384]{1,0:T(8,128)(2,1)S(1)}, u32[]{:S(2)}, u32[]{:S(2)}) collective-permute-start(bf16[192,384]{1,0:T(8,128)(2,1)S(1)} %get-tuple-element.133), channel_id=1, source_target_pairs={{0,32},{16,48},{32,0},{48,16},{64,96},{80,112},{96,64},{112,80},{1... | collective-permute-start | bytes 442376 | tf_op jit(solution)/shard_map/ppermute | solution.py:58
  256.3 10.4 %collective-permute-start.62 = (f32[24,512]{1,0:T(8,128)S(1)}, f32[24,512]{1,0:T(8,128)S(1)}, u32[]{:S(2)}, u32[]{:S(2)}) collective-permute-start(f32[24,512]{1,0:T(8,128)S(1)} %add.109), channel_id=1, source_target_pairs={{0,16},{16,0},{32,48},{48,32},{64,80},{80,64},{96,112},{112,96},{1... | collective-permute-start | bytes 147464 | tf_op jit(solution)/shard_map/ppermute | solution.py:58
  257.7 12.0 %collective-permute-start.45 = (bf16[192,384]{1,0:T(8,128)(2,1)S(1)}, bf16[192,384]{1,0:T(8,128)(2,1)S(1)}, u32[]{:S(2)}, u32[]{:S(2)}) collective-permute-start(bf16[192,384]{1,0:T(8,128)(2,1)S(1)} %get-tuple-element.134), channel_id=1, source_target_pairs={{0,48},{16,32},{32,16},{48,0},{64,112},{80,96},{96,80},{112,64},{1... | collective-permute-start | bytes 442376 | tf_op jit(solution)/shard_map/ppermute | solution.py:58
  260.4 10.8 %collective-permute-start.46 = (bf16[192,384]{1,0:T(8,128)(2,1)S(1)}, bf16[192,384]{1,0:T(8,128)(2,1)S(1)}, u32[]{:S(2)}, u32[]{:S(2)}) collective-permute-start(bf16[192,384]{1,0:T(8,128)(2,1)S(1)} %get-tuple-element.135), channel_id=1, source_target_pairs={{0,64},{16,80},{32,96},{48,112},{64,0},{80,16},{96,32},{112,48},{1... | collective-permute-start | bytes 442376 | tf_op jit(solution)/shard_map/ppermute | solution.py:58
  262.9 8.3 %collective-permute-start.47 = (bf16[192,384]{1,0:T(8,128)(2,1)S(1)}, bf16[192,384]{1,0:T(8,128)(2,1)S(1)}, u32[]{:S(2)}, u32[]{:S(2)}) collective-permute-start(bf16[192,384]{1,0:T(8,128)(2,1)S(1)} %get-tuple-element.136), channel_id=1, source_target_pairs={{0,80},{16,64},{32,112},{48,96},{64,16},{80,0},{96,48},{112,32},{1... | collective-permute-start | bytes 442376 | tf_op jit(solution)/shard_map/ppermute | solution.py:58
  264.7 8.9 %collective-permute-start.48 = (bf16[192,384]{1,0:T(8,128)(2,1)S(1)}, bf16[192,384]{1,0:T(8,128)(2,1)S(1)}, u32[]{:S(2)}, u32[]{:S(2)}) collective-permute-start(bf16[192,384]{1,0:T(8,128)(2,1)S(1)} %get-tuple-element.137), channel_id=1, source_target_pairs={{0,96},{16,112},{32,64},{48,80},{64,32},{80,48},{96,0},{112,16},{1... | collective-permute-start | bytes 442376 | tf_op jit(solution)/shard_map/ppermute | solution.py:58
  266.7 8.7 %collective-permute-start.49 = (bf16[192,384]{1,0:T(8,128)(2,1)S(1)}, bf16[192,384]{1,0:T(8,128)(2,1)S(1)}, u32[]{:S(2)}, u32[]{:S(2)}) collective-permute-start(bf16[192,384]{1,0:T(8,128)(2,1)S(1)} %get-tuple-element.138), channel_id=1, source_target_pairs={{0,112},{16,96},{32,80},{48,64},{64,48},{80,32},{96,16},{112,0},{1... | collective-permute-start | bytes 442376 | tf_op jit(solution)/shard_map/ppermute | solution.py:58
  (69 other events, 1605.1 us)
